TPU v7x, 128 devices: a whole 4x4x4 slice. The times are simulated.
128 devices in a mesh: ctx: 16 (over x_lo, y, core), fsdp: 8 (over z, x_hi).
Axes of the slice: x: 4 (x_hi: 2, x_lo: 2; x = x_hi * 2 + x_lo), y: 4, z: 4, core: 2. Of those that a mesh axis runs over, the one named last changes fastest.
Arguments:
- block_input: bfloat16 [8, 2, 1024, 1152], P('fsdp', None, 'ctx'), may hold values from -6 to 6
- doc_ids: int32 [8, 2, 1024], P('fsdp', None, 'ctx'), may hold values from 0 to 3, as said below
- positions: int32 [8, 2, 1024], P('fsdp', None, 'ctx'), may hold values from 0 to 1023
- qkv_weight: bfloat16 [1152, 1536], P('fsdp')
- out_weight: bfloat16 [1024, 1152], P('fsdp'), may hold values from -0.1875 to 0.1875
- gate_up_weight: bfloat16 [1152, 13824], P('fsdp'), may hold values from -0.1875 to 0.1875
- down_weight: bfloat16 [6912, 1152], P('fsdp'), may hold values from -0.078125 to 0.078125
- scale_attn_in: float32 [1152], replicated, may hold values from 0.1 to 1.9
- scale_attn_out: float32 [1152], replicated, may hold values from 0.1 to 1.9
- scale_ff_in: float32 [1152], replicated, may hold values from 0.1 to 1.9
- scale_ff_out: float32 [1152], replicated, may hold values from 0.1 to 1.9
- scale_query: float32 [256], replicated, may hold values from 0.5 to 4.5
- scale_key: float32 [256], replicated, may hold values from 0.5 to 4.5
- grad_output: bfloat16 [8, 2, 1024, 1152], P('fsdp', None, 'ctx'), may hold values from -6 to 6
Outputs:
- block_output: bfloat16 [8, 2, 1024, 1152], P('fsdp', None, 'ctx')
- input_grad: float32 [8, 2, 1024, 1152], P('fsdp', None, 'ctx')
- qkv_grad: float32 [1152, 1536], P(None, ('ctx', 'fsdp'))
- out_grad: float32 [1024, 1152], P(('ctx', 'fsdp'))
- gate_up_grad: float32 [1152, 13824], P(None, ('ctx', 'fsdp'))
- down_grad: float32 [6912, 1152], P(('ctx', 'fsdp'))
- attn_in_grad: float32 [1152], replicated
- attn_out_grad: float32 [1152], replicated
- ff_in_grad: float32 [1152], replicated
- ff_out_grad: float32 [1152], replicated
- query_gain_grad: float32 [256], replicated
- key_gain_grad: float32 [256], replicated
Inputs may be any that keep to these rules, and one draw needn't show every extreme that they name: `doc_ids`: within each sequence document numbers start at 0 and never fall; a token's position is its distance from the first token of its document. The last sequence of each pair is one document; every other sequence holds exactly 4 documents.
All inputs are finite; a program needn't handle non-finite values.
Results may differ from a plain program's by a relative error of at most 0.02.
The roundings to bfloat16 on the way count: a program that leaves them out, or rounds other values in their place, can miss the bound.
Values may be sent and summed in bfloat16 or wider, within the bound.
A program may use at most 384 MiB of HBM per device.

v0:
```python
import jax
import jax.numpy as jnp
from jax import lax
from jax.sharding import PartitionSpec as P

D = 1152
FF = 6912
HEADS = 4
HEAD_DIM = 256


NORM_EPS = 1e-06
ROPE_BASE = 1000000.0
GELU_COEF = 0.7978845608028654
GELU_CUBIC = 0.044715
MASK_FLOOR = -1e30


def rms_scale(tensor):
    return lax.rsqrt(jnp.mean(tensor * tensor, axis=-1, keepdims=True) + NORM_EPS)


def norm_back(tensor, scaled, gain_vector, cotangent):
    weighted = cotangent * gain_vector
    inner_mean = jnp.mean(weighted * tensor, axis=-1, keepdims=True)
    return scaled * (weighted - tensor * scaled * scaled * inner_mean)


def rope_tables(positions):
    half_width = HEAD_DIM // 2
    frequency = ROPE_BASE ** (-2.0 * jnp.arange(half_width, dtype=jnp.float32) / HEAD_DIM)
    angles = positions.astype(jnp.float32)[..., None] * frequency
    return (jnp.cos(angles), jnp.sin(angles))


def rotate(tensor, cosine, sine_part):
    half_width = tensor.shape[-1] // 2
    leading = tensor[..., :half_width]
    trailing = tensor[..., half_width:]
    return jnp.concatenate(
        [leading * cosine - trailing * sine_part, trailing * cosine + leading * sine_part], axis=-1
    )


def rotate_back(cotangent, cosine, sine_part):
    half_width = cotangent.shape[-1] // 2
    leading = cotangent[..., :half_width]
    trailing = cotangent[..., half_width:]
    return jnp.concatenate(
        [leading * cosine + trailing * sine_part, trailing * cosine - leading * sine_part], axis=-1
    )


def gelu_parts(gate_part):
    tanh_input = GELU_COEF * (gate_part + GELU_CUBIC * gate_part * gate_part * gate_part)
    tanh_value = jnp.tanh(tanh_input)
    gelu_value = 0.5 * gate_part * (1.0 + tanh_value)
    gelu_slope = 0.5 * (1.0 + tanh_value) + 0.5 * gate_part * (
        1.0 - tanh_value * tanh_value
    ) * GELU_COEF * (1.0 + 3.0 * GELU_CUBIC * gate_part * gate_part)
    return (gelu_value, gelu_slope)


def allowed_mask(query_pos, query_doc, key_pos, key_doc):
    same_doc = query_doc[:, :, None, None] == key_doc[:, None, None, :]
    causal = key_pos[:, None, None, :] <= query_pos[:, :, None, None]
    return same_doc & causal


def transposed_product(right_rows, pieces):
    return lax.dot_general(
        right_rows, pieces, (((1,), (1,)), ((), ())), preferred_element_type=jnp.float32
    )


def transposed_left(left_rows, right_rows):
    return lax.dot_general(
        left_rows, right_rows, (((0,), (0,)), ((), ())), preferred_element_type=jnp.float32
    )


def add_product(left_rows, pieces):
    return jnp.dot(left_rows, pieces, preferred_element_type=jnp.float32)


def fold_grads(exchanged, pieces):
    cuts = [member for member in exchanged]
    return (
        transposed_left(pieces[0], cuts[0]),
        transposed_left(pieces[1], cuts[1]),
        transposed_left(cuts[2], pieces[2]),
        transposed_left(cuts[3], pieces[3]),
    )


def attention_forward(queries, key_rows, value_rows, allowed, score_scale):
    scores = (
        jnp.einsum("bshd,bnd->bshn", queries, key_rows, preferred_element_type=jnp.float32)
        * score_scale
    )
    masked = jnp.where(allowed, scores, MASK_FLOOR)
    best_score = jnp.max(masked, axis=-1)
    weights = jnp.where(allowed, jnp.exp(scores - best_score[..., None]), 0.0)
    totals = jnp.sum(weights, axis=-1)
    attended = (
        jnp.einsum(
            "bshn,bnd->bshd",
            weights,
            value_rows.astype(jnp.float32),
            precision=lax.Precision.HIGHEST,
        )
        / totals[..., None]
    )
    return (attended, best_score + jnp.log(totals))


def attention_backward(
    queries, key_rows, value_rows, allowed, score_scale, log_total, attended, attended_cot
):
    scores = (
        jnp.einsum("bshd,bnd->bshn", queries, key_rows, preferred_element_type=jnp.float32)
        * score_scale
    )
    probabilities = jnp.where(allowed, jnp.exp(scores - log_total[..., None]), 0.0)
    row_delta = jnp.sum(attended_cot.astype(jnp.float32) * attended, axis=-1)
    prob_cot = jnp.einsum(
        "bshd,bnd->bshn", attended_cot, value_rows, preferred_element_type=jnp.float32
    )
    score_cot = (probabilities * (prob_cot - row_delta[..., None])).astype(jnp.bfloat16)
    query_cot = (
        jnp.einsum("bshn,bnd->bshd", score_cot, key_rows, preferred_element_type=jnp.float32)
        * score_scale
    )
    key_cot = (
        jnp.einsum("bshn,bshd->bnd", score_cot, queries, preferred_element_type=jnp.float32)
        * score_scale
    )
    value_cot = jnp.einsum(
        "bshn,bshd->bnd",
        probabilities.astype(jnp.bfloat16),
        attended_cot,
        preferred_element_type=jnp.float32,
    )
    return (query_cot, key_cot, value_cot)


def on_device(
    block_input,
    doc_ids,
    positions,
    qkv_weight,
    out_weight,
    gate_up_weight,
    down_weight,
    scale_attn_in,
    scale_attn_out,
    scale_ff_in,
    scale_ff_out,
    scale_query,
    scale_key,
    grad_output,
):
    seq_count = block_input.shape[1]
    seq_rows = block_input.shape[2]
    row_count = seq_count * seq_rows
    head_total = HEADS * HEAD_DIM
    score_scale = HEAD_DIM ** (-0.5)
    qkv_full, out_full = (
        lax.all_gather(qkv_weight, "fsdp", axis=0, tiled=True),
        lax.all_gather(out_weight, "fsdp", axis=0, tiled=True),
    )
    resid_in = block_input.reshape(row_count, D).astype(jnp.float32)
    scale_one = rms_scale(resid_in)
    attn_input = (resid_in * scale_one * scale_attn_in).astype(jnp.bfloat16)
    projected_qkv = jnp.dot(attn_input, qkv_full, preferred_element_type=jnp.float32)
    query_raw = projected_qkv[:, :head_total].reshape(row_count, HEADS, HEAD_DIM)
    key_raw = projected_qkv[:, head_total : head_total + HEAD_DIM]
    value_rows = projected_qkv[:, head_total + HEAD_DIM :].astype(jnp.bfloat16)
    query_scale = rms_scale(query_raw)
    key_scale = rms_scale(key_raw)
    local_pos = positions.reshape(seq_count, seq_rows)
    local_doc = doc_ids.reshape(seq_count, seq_rows)
    cosine, sine_part = rope_tables(local_pos.reshape(row_count))
    queries = rotate(
        query_raw * query_scale * scale_query, cosine[:, None, :], sine_part[:, None, :]
    ).astype(jnp.bfloat16)
    key_rows = rotate(key_raw * key_scale * scale_key, cosine, sine_part).astype(jnp.bfloat16)
    key_all, value_all, pos_all, doc_all = (
        lax.all_gather(key_rows.reshape(seq_count, seq_rows, HEAD_DIM), "ctx", axis=1, tiled=True),
        lax.all_gather(
            value_rows.reshape(seq_count, seq_rows, HEAD_DIM), "ctx", axis=1, tiled=True
        ),
        lax.all_gather(local_pos, "ctx", axis=1, tiled=True),
        lax.all_gather(local_doc, "ctx", axis=1, tiled=True),
    )
    allowed = allowed_mask(local_pos, local_doc, pos_all, doc_all)
    query_blocks = queries.reshape(seq_count, seq_rows, HEADS, HEAD_DIM)
    attended, log_total = attention_forward(query_blocks, key_all, value_all, allowed, score_scale)
    attended_low = attended.reshape(row_count, head_total).astype(jnp.bfloat16)
    projected = jnp.dot(attended_low, out_full, preferred_element_type=jnp.float32)
    scale_two = rms_scale(projected)
    middle = resid_in + projected * scale_two * scale_attn_out
    scale_three = rms_scale(middle)
    ff_input = (middle * scale_three * scale_ff_in).astype(jnp.bfloat16)
    gate_up = add_product(ff_input, lax.all_gather(gate_up_weight, "fsdp", axis=0, tiled=True))
    gate_part = gate_up[:, :FF]
    up_part = gate_up[:, FF:]
    gelu_value, gelu_slope = gelu_parts(gate_part)
    activation = (gelu_value * up_part).astype(jnp.bfloat16)
    down_out = add_product(activation, lax.all_gather(down_weight, "fsdp", axis=0, tiled=True))
    scale_four = rms_scale(down_out)
    block_output = (middle + down_out * scale_four * scale_ff_out).astype(jnp.bfloat16)
    cotangent = grad_output.reshape(row_count, D).astype(jnp.float32)
    ff_out_grad = jnp.sum(cotangent * down_out * scale_four, axis=0)
    down_cot = norm_back(down_out, scale_four, scale_ff_out, cotangent).astype(jnp.bfloat16)
    act_cot = transposed_product(down_cot, lax.all_gather(down_weight, "fsdp", axis=0, tiled=True))
    gate_up_cot = jnp.concatenate(
        [act_cot * up_part * gelu_slope, act_cot * gelu_value], axis=1
    ).astype(jnp.bfloat16)
    ff_input_cot = transposed_product(
        gate_up_cot, lax.all_gather(gate_up_weight, "fsdp", axis=0, tiled=True)
    )
    ff_in_grad = jnp.sum(ff_input_cot * middle * scale_three, axis=0)
    middle_cot = cotangent + norm_back(middle, scale_three, scale_ff_in, ff_input_cot)
    attn_out_grad = jnp.sum(middle_cot * projected * scale_two, axis=0)
    projected_cot = norm_back(projected, scale_two, scale_attn_out, middle_cot).astype(jnp.bfloat16)
    attended_cot = transposed_product(projected_cot, out_full).astype(jnp.bfloat16)
    query_cot, key_cot, value_cot = attention_backward(
        query_blocks,
        key_all,
        value_all,
        allowed,
        score_scale,
        log_total,
        attended,
        attended_cot.reshape(seq_count, seq_rows, HEADS, HEAD_DIM),
    )
    kv_local = lax.psum_scatter(
        jnp.concatenate([key_cot, value_cot], axis=2).astype(jnp.bfloat16),
        "ctx",
        scatter_dimension=1,
        tiled=True,
    ).astype(jnp.float32)
    key_cot_local = kv_local[:, :, :HEAD_DIM].reshape(row_count, HEAD_DIM)
    value_cot_local = kv_local[:, :, HEAD_DIM:].reshape(row_count, HEAD_DIM)
    query_back = rotate_back(
        query_cot.reshape(row_count, HEADS, HEAD_DIM), cosine[:, None, :], sine_part[:, None, :]
    )
    key_back = rotate_back(key_cot_local, cosine, sine_part)
    query_gain_grad = jnp.sum(query_back * query_raw * query_scale, axis=(0, 1))
    key_gain_grad = jnp.sum(key_back * key_raw * key_scale, axis=0)
    qkv_cot = jnp.concatenate(
        [
            norm_back(query_raw, query_scale, scale_query, query_back).reshape(
                row_count, head_total
            ),
            norm_back(key_raw, key_scale, scale_key, key_back),
            value_cot_local,
        ],
        axis=1,
    ).astype(jnp.bfloat16)
    attn_input_cot = transposed_product(qkv_cot, qkv_full)
    attn_in_grad = jnp.sum(attn_input_cot * resid_in * scale_one, axis=0)
    input_grad = middle_cot + norm_back(resid_in, scale_one, scale_attn_in, attn_input_cot)
    gain_sums = lax.psum(
        (attn_in_grad, attn_out_grad, ff_in_grad, ff_out_grad, query_gain_grad, key_gain_grad),
        ("ctx", "fsdp"),
    )
    exchanged = (
        lax.all_to_all(qkv_cot, ("ctx", "fsdp"), split_axis=1, concat_axis=0, tiled=True),
        lax.all_to_all(gate_up_cot, ("ctx", "fsdp"), split_axis=1, concat_axis=0, tiled=True),
        lax.all_to_all(attended_low, ("ctx", "fsdp"), split_axis=1, concat_axis=0, tiled=True),
        lax.all_to_all(activation, ("ctx", "fsdp"), split_axis=1, concat_axis=0, tiled=True),
    )
    qkv_grad, gate_up_grad, out_grad, down_grad = fold_grads(
        exchanged,
        (
            lax.all_gather(attn_input, ("ctx", "fsdp"), axis=0, tiled=True),
            lax.all_gather(ff_input, ("ctx", "fsdp"), axis=0, tiled=True),
            lax.all_gather(projected_cot, ("ctx", "fsdp"), axis=0, tiled=True),
            lax.all_gather(down_cot, ("ctx", "fsdp"), axis=0, tiled=True),
        ),
    )
    return (
        block_output.reshape(1, seq_count, seq_rows, D),
        input_grad.reshape(1, seq_count, seq_rows, D),
        qkv_grad,
        out_grad,
        gate_up_grad,
        down_grad,
        gain_sums[0],
        gain_sums[1],
        gain_sums[2],
        gain_sums[3],
        gain_sums[4],
        gain_sums[5],
    )


def solution(mesh):
    return jax.shard_map(
        on_device,
        mesh=mesh,
        in_specs=(
            P("fsdp", None, "ctx", None),
            P("fsdp", None, "ctx"),
            P("fsdp", None, "ctx"),
            P("fsdp", None),
            P("fsdp", None),
            P("fsdp", None),
            P("fsdp", None),
            P(),
            P(),
            P(),
            P(),
            P(),
            P(),
            P("fsdp", None, "ctx", None),
        ),
        out_specs=(
            P("fsdp", None, "ctx", None),
            P("fsdp", None, "ctx", None),
            P(None, ("ctx", "fsdp")),
            P(("ctx", "fsdp"), None),
            P(None, ("ctx", "fsdp")),
            P(("ctx", "fsdp"), None),
            P(),
            P(),
            P(),
            P(),
            P(),
            P(),
        ),
        check_vma=False,
    )
```

profile of v0, /device:TPU:14, one launch (start us, length us, event | category | flops | bytes accessed | tf_op | source)
XLA Modules:
  0.0 2267.3 jit_solution(3583112399514239907)
XLA Ops:
  11.9 66.1 %all-gather.13.cloned.1.call-done = bf16[1152,1536]{1,0:T(8,128)(2,1)} async-done(((bf16[144,1536]{1,0:T(8,128)(2,1)}), bf16[1152,1536]{1,0:T(8,128)(2,1)}) %all-gather.13.cloned.1.call-update) | async-done | bytes 3538960 | tf_op jit(solution)/shard_map/all_gather | solution.py:169
  85.2 18.5 all-gather.1
  104.0 19.0 all-gather
  128.1 20.4 all-gather.17.cloned.1.call-done
  148.5 4.2 fusion.79
  153.0 53.5 %all-gather.19.cloned.1.call-done = bf16[1024,1152]{1,0:T(8,128)(2,1)} async-done(((bf16[128,1152]{1,0:T(8,128)(2,1)}), bf16[1024,1152]{1,0:T(8,128)(2,1)}) %all-gather.19.cloned.1.call-update) | async-done | bytes 2359312 | tf_op jit(solution)/shard_map/all_gather | solution.py:170
  210.9 314.5 %all-gather.21.cloned.1.call-done = bf16[1152,13824]{1,0:T(8,128)(2,1)} async-done(((bf16[144,13824]{1,0:T(8,128)(2,1)}), bf16[1152,13824]{1,0:T(8,128)(2,1)}) %all-gather.21.cloned.1.call-update) | async-done | bytes 31850512 | tf_op jit(solution)/shard_map/all_gather | solution.py:205
  525.4 13.2 fusion.81
  543.0 157.7 %all-gather.23.cloned.1.call-done = bf16[6912,1152]{1,0:T(8,128)(2,1)} async-done(((bf16[864,1152]{1,0:T(8,128)(2,1)}), bf16[6912,1152]{1,0:T(8,128)(2,1)}) %all-gather.23.cloned.1.call-update) | async-done | bytes 15925264 | tf_op jit(solution)/shard_map/all_gather | solution.py:210
  700.6 8.1 multiply_reduce_fusion.4
  710.7 11.4 fusion.6
  722.1 17.0 multiply_reduce_fusion
  751.7 6.2 copy.152
  770.1 7.4 all-to-all-start.3
  783.1 111.8 %all-reduce.4.cloned.1.call-done = bf16[2,1024,512]{2,0,1:T(2,128)(2,1)} async-done(((bf16[2,1024,512]{2,0,1:T(2,128)(2,1)}), bf16[2,1024,512]{2,0,1:T(2,128)(2,1)}) %all-reduce.4.cloned.1.call-update) | async-done | bytes 2097168
  901.6 13.6 all-to-all-start
  915.2 9.6 reshape.290
  924.8 10.2 reshape.289
  938.1 4.5 copy.168
  942.6 3.7 pad_maximum_fusion
  946.3 10.2 all-to-all-start.2
  966.4 96.3 %all-reduce.1 = (f32[1152]{0:T(1024)}, f32[1152]{0:T(1024)}, f32[1152]{0:T(1024)}, f32[1152]{0:T(1024)}, f32[256]{0:T(256)}, /*index=5*/f32[256]{0:T(256)}) all-reduce(f32[1152]{0:T(1024)S(1)} %get-tuple-element.20, f32[1152]{0:T(1024)S(1)} %copy-done.48, ...), channel_id=1, replica_groups=mesh['ctx'=16,'fsdp'=8] {'ctx','fsdp'}, use_global_device_ids=true, to_apply=%region_17.18 | all-reduce | flops 5120 | bytes 40960 | tf_op jit(solution)/shard_map/psum | solution.py:265
  1066.4 8.6 all-to-all-start.1
  1078.5 4.9 copy.178
  1083.5 91.6 %all-gather.25.cloned.1.call-done = bf16[16384,1152]{1,0:T(8,128)(2,1)} async-done(((bf16[128,1152]{1,0:T(8,128)(2,1)}), bf16[16384,1152]{1,0:T(8,128)(2,1)}) %all-gather.25.cloned.1.call-update) | async-done | bytes 37748752 | tf_op jit(solution)/shard_map/all_gather | solution.py:278
  1175.0 15.1 fusion.82
  1190.1 343.3 %all-gather.29.cloned.1.call-done = bf16[16384,1152]{1,0:T(8,128)(2,1)} async-done(((bf16[128,1152]{1,0:T(8,128)(2,1)}), bf16[16384,1152]{1,0:T(8,128)(2,1)}) %all-gather.29.cloned.1.call-update) | async-done | bytes 37748752 | tf_op jit(solution)/shard_map/all_gather | solution.py:279
  1533.3 19.0 fusion.83
  1552.4 336.2 %all-gather.27.cloned.1.call-done = bf16[16384,1152]{1,0:T(8,128)(2,1)} async-done(((bf16[128,1152]{1,0:T(8,128)(2,1)}), bf16[16384,1152]{1,0:T(8,128)(2,1)}) %all-gather.27.cloned.1.call-update) | async-done | bytes 37748752 | tf_op jit(solution)/shard_map/all_gather | solution.py:280
  1888.6 14.9 fusion.54
  1903.5 340.5 %all-gather.31.cloned.1.call-done = bf16[16384,1152]{1,0:T(8,128)(2,1)} async-done(((bf16[128,1152]{1,0:T(8,128)(2,1)}), bf16[16384,1152]{1,0:T(8,128)(2,1)}) %all-gather.31.cloned.1.call-update) | async-done | bytes 37748752 | tf_op jit(solution)/shard_map/all_gather | solution.py:281
  2244.0 15.5 fusion.84
  (262 shorter events, 82.9 us)
Async XLA Ops:
  8.0 73.4 %copy-start.50 = (f32[256]{0:T(256)S(1)}, f32[256]{0:T(256)}, u32[]{:S(2)}) copy-start(f32[256]{0:T(256)} %param.26) | copy-start | bytes 3076
  8.0 70.0 %all-gather.13.cloned.1.call-start = ((), (), s32[]{:S(2)}) async-start(), calls=%async_computation.4 | async-start | bytes 3981312 | tf_op jit(solution)/shard_map/all_gather | solution.py:169
  8.8 115.5 %all-gather.15.cloned.1.call-start = ((), (), s32[]{:S(2)}) async-start(), calls=%async_computation.5 | async-start | bytes 1114112 | tf_op jit(solution)/shard_map/all_gather | solution.py:189
  9.6 74.9 %copy-start.60 = (f32[128]{0:T(128)}, f32[128]{0:T(128)S(1)}, u32[]{:S(2)}) copy-start(f32[128]{0:T(128)S(1)} %convert_element_type.89) | copy-start | bytes 1540
  10.8 70.0 %copy-start.64 = (f32[128]{0:T(128)}, f32[128]{0:T(128)S(1)}, u32[]{:S(2)}) copy-start(f32[128]{0:T(128)S(1)} %rsqrt.52) | copy-start | bytes 1540
  10.8 73.6 %copy-start.62 = (f32[128]{0:T(128)}, f32[128]{0:T(128)S(1)}, u32[]{:S(2)}) copy-start(f32[128]{0:T(128)S(1)} %multiply_power_fusion) | copy-start | bytes 1540
  11.9 72.5 %copy-start.22 = (bf16[128,1152]{1,0:T(8,128)(2,1)}, bf16[128,1152]{1,0:T(8,128)(2,1)S(1)}, u32[]{:S(2)}) copy-start(bf16[128,1152]{1,0:T(8,128)(2,1)S(1)} %fusion.39) | copy-start | bytes 884740
  82.5 66.0 %all-gather.17.cloned.1.call-start = ((), (), s32[]{:S(2)}) async-start(), calls=%async_computation.6 | async-start | bytes 1114112 | tf_op jit(solution)/shard_map/all_gather | solution.py:190
  83.2 123.3 %all-gather.19.cloned.1.call-start = ((), (), s32[]{:S(2)}) async-start(), calls=%async_computation.7 | async-start | bytes 2654208 | tf_op jit(solution)/shard_map/all_gather | solution.py:170
  83.8 441.6 %all-gather.21.cloned.1.call-start = ((), (), s32[]{:S(2)}) async-start(), calls=%async_computation.8 | async-start | bytes 35831808 | tf_op jit(solution)/shard_map/all_gather | solution.py:205
  84.5 616.2 %all-gather.23.cloned.1.call-start = ((), (), s32[]{:S(2)}) async-start(), calls=%async_computation.9 | async-start | bytes 17915904 | tf_op jit(solution)/shard_map/all_gather | solution.py:210
  85.0 809.9 %all-reduce.4.cloned.1.call-start = ((), (), s32[]{:S(2)}) async-start(), calls=%async_computation.14 | async-start | bytes 4194304
  152.7 58.2 %copy-start.26 = (bf16[2,64,4,256]{3,1,2,0:T(8,128)(2,1)}, bf16[2,64,4,256]{3,1,2,0:T(8,128)(2,1)S(1)}, u32[]{:S(2)}) copy-start(bf16[2,64,4,256]{3,1,2,0:T(8,128)(2,1)S(1)} %get-tuple-element.51) | copy-start | bytes 786436
  152.7 56.9 %copy-start.13 = (bf16[1,2,64,1152]{3,2,1,0:T(8,128)(2,1)S(1)}, bf16[1,2,64,1152]{3,2,1,0:T(8,128)(2,1)}, u32[]{:S(2)}) copy-start(bf16[1,2,64,1152]{3,2,1,0:T(8,128)(2,1)} %param.14) | copy-start | bytes 884740
  152.7 56.9 %copy-start.43 = (f32[1152]{0:T(1024)S(1)}, f32[1152]{0:T(1024)}, u32[]{:S(2)}) copy-start(f32[1152]{0:T(1024)} %param.22) | copy-start | bytes 13828
  152.7 58.0 %copy-start.45 = (f32[1152]{0:T(1024)S(1)}, f32[1152]{0:T(1024)}, u32[]{:S(2)}) copy-start(f32[1152]{0:T(1024)} %param.23) | copy-start | bytes 13828
  210.9 314.5 %copy-start.19 = (bf16[128,1152]{1,0:T(8,128)(2,1)}, bf16[128,1152]{1,0:T(8,128)(2,1)S(1)}, u32[]{:S(2)}) copy-start(bf16[128,1152]{1,0:T(8,128)(2,1)S(1)} %multiply_convert_fusion.4) | copy-start | bytes 884740
  542.9 165.8 %copy-start.44 = (f32[1152]{0:T(1024)S(1)}, f32[1152]{0:T(1024)}, u32[]{:S(2)}) copy-start(f32[1152]{0:T(1024)} %param.24) | copy-start | bytes 13828
  542.9 166.6 %copy-start.2 = (f32[128,1152]{1,0:T(8,128)S(1)}, f32[128,1152]{1,0:T(8,128)}, u32[]{:S(2)}) copy-start(f32[128,1152]{1,0:T(8,128)} %copy-done.1) | copy-start | bytes 1769476
  757.9 417.1 %all-gather.25.cloned.1.call-start = ((), (), s32[]{:S(2)}) async-start(), calls=%async_computation.10 | async-start | bytes 38043648 | tf_op jit(solution)/shard_map/all_gather | solution.py:278
  758.5 774.9 %all-gather.29.cloned.1.call-start = ((), (), s32[]{:S(2)}) async-start(), calls=%async_computation.12 | async-start | bytes 38043648 | tf_op jit(solution)/shard_map/all_gather | solution.py:279
  759.1 1129.5 %all-gather.27.cloned.1.call-start = ((), (), s32[]{:S(2)}) async-start(), calls=%async_computation.11 | async-start | bytes 38043648 | tf_op jit(solution)/shard_map/all_gather | solution.py:280
  759.6 1484.4 %all-gather.31.cloned.1.call-start = ((), (), s32[]{:S(2)}) async-start(), calls=%async_computation.13 | async-start | bytes 38043648 | tf_op jit(solution)/shard_map/all_gather | solution.py:281
  770.1 130.2 %all-to-all-start.3 = ((bf16[128,128,54]{0,2,1:T(8,128)(2,1)}), bf16[128,128,54]{0,2,1:T(8,128)(2,1)S(1)}, u32[]{:S(2)}, u32[]{:S(2)}) async-start(bf16[128,128,54]{0,2,1:T(8,128)(2,1)} %all_to_all.59), calls=%async_computation.3 | async-start | bytes 3670016 | tf_op jit(solution)/shard_map/all_to_all | solution.py:273
  779.5 116.6 %copy-start.61 = (f32[128]{0:T(128)S(1)}, f32[128]{0:T(128)}, u32[]{:S(2)}) copy-start(f32[128]{0:T(128)} %copy-done.60) | copy-start | bytes 1540
  779.5 116.6 %copy-start.63 = (f32[128]{0:T(128)S(1)}, f32[128]{0:T(128)}, u32[]{:S(2)}) copy-start(f32[128]{0:T(128)} %copy-done.62) | copy-start | bytes 1540
  779.5 116.9 %copy-start.51 = (f32[256]{0:T(256)S(1)}, f32[256]{0:T(256)}, u32[]{:S(2)}) copy-start(f32[256]{0:T(256)} %param.26) | copy-start | bytes 3076
  779.5 116.9 %copy-start.57 = (f32[128]{0:T(128)S(1)}, f32[128]{0:T(128)}, u32[]{:S(2)}) copy-start(f32[128]{0:T(128)} %copy-done.56) | copy-start | bytes 1540
  901.6 44.7 %all-to-all-start = ((bf16[128,128,12]{0,2,1:T(8,128)(2,1)}), bf16[128,128,12]{0,2,1:T(8,128)(2,1)}, u32[]{:S(2)}, u32[]{:S(2)}) async-start(bf16[128,128,12]{0,2,1:T(8,128)(2,1)} %convert_element_type.105), calls=%async_computation | async-start | bytes 1048576 | tf_op jit(solution)/shard_map/all_to_all | solution.py:270
  946.3 120.1 %all-to-all-start.2 = ((bf16[128,128,108]{0,2,1:T(8,128)(2,1)}), bf16[128,128,108]{0,2,1:T(8,128)(2,1)}, u32[]{:S(2)}, u32[]{:S(2)}) async-start(bf16[128,128,108]{0,2,1:T(8,128)(2,1)} %pad_maximum_fusion), calls=%async_computation.2 | async-start | bytes 7340032 | tf_op jit(solution)/shard_map/all_to_all | solution.py:271
  964.3 98.4 %copy-start.12 = (f32[128,1152]{1,0:T(8,128)S(1)}, f32[128,1152]{1,0:T(8,128)}, u32[]{:S(2)}) copy-start(f32[128,1152]{1,0:T(8,128)} %copy-done.11) | copy-start | bytes 1769476
  1066.4 486.0 %all-to-all-start.1 = ((bf16[128,128,8]{0,2,1:T(8,128)(2,1)}), bf16[128,128,8]{0,2,1:T(8,128)(2,1)S(1)}, u32[]{:S(2)}, u32[]{:S(2)}) async-start(bf16[128,128,8]{0,2,1:T(8,128)(2,1)} %convert_element_type.106), calls=%async_computation.1 | async-start | bytes 524288 | tf_op jit(solution)/shard_map/all_to_all | solution.py:272
  (51 other events, 430.3 us)
Sparse Core Ops, SparseCore 0:
  11.2 66.7 all-gather.12
  82.6 30.9 all-gather.14
  115.9 32.6 all-gather.16
  150.7 55.8 all-gather.18
  208.7 316.6 all-gather.20
  527.6 173.0 all-gather.22
  758.0 136.9 all-reduce.3
Sparse Core Ops, SparseCore 1:
  760.1 414.9 all-gather.24
  1176.6 356.7 all-gather.28
  1534.9 353.6 all-gather.26
  1890.3 353.6 all-gather.30
where the time goes:
time: 2280 us; the launch traced here: 2270 us
  waiting for transfers between devices  1840 us (81%)
  matrix products  136 us (6%)
  blocking collectives  134 us (6%)
  local copies, waits for them, and re-layouts  73.5 us (3%)
  starting transfers between devices  40.2 us (2%)
  other arithmetic  26.1 us (1%)
    all_gather x1, waiting for transfers between devices, on_device(): lax.all_gather(ff_input, ('ctx', 'fsdp'), axis=0, tiled=True)  343 us
    all_gather x1, waiting for transfers between devices, on_device(): lax.all_gather(down_cot, ('ctx', 'fsdp'), axis=0, tiled=True)  341 us
    all_gather x1, waiting for transfers between devices, on_device(): lax.all_gather(projected_cot, ('ctx', 'fsdp'), axis=0, tiled=True)  336 us
    all_gather x1, waiting for transfers between devices, on_device(): lax.all_gather(gate_up_weight, 'fsdp', axis=0, tiled=True)  315 us
    all_gather x1, waiting for transfers between devices, on_device(): lax.all_gather(down_weight, 'fsdp', axis=0, tiled=True)  158 us
    unnamed x12, waiting for transfers between devices  116 us
    psum x1, blocking collectives, on_device(): lax.psum((attn_in_grad, attn_out_grad, ff_in_grad, ff_out_grad, query_gai...  96.3 us
    all_gather x1, waiting for transfers between devices, on_device(): lax.all_gather(attn_input, ('ctx', 'fsdp'), axis=0, tiled=True)  91.6 us
  transfers between devices with their start and end apart: 15, of which 10 were waited for; matrix products, arithmetic and copies ran while one was open for 7% of the time, Pallas kernels for 0%

commit v1 on v0

--- a/solution.py
+++ b/solution.py
@@ -61,10 +61,10 @@
     return (gelu_value, gelu_slope)
 
 
-def allowed_mask(query_pos, query_doc, key_pos, key_doc):
-    same_doc = query_doc[:, :, None, None] == key_doc[:, None, None, :]
-    causal = key_pos[:, None, None, :] <= query_pos[:, :, None, None]
-    return same_doc & causal
+def allowed_mask(query_pos, query_index, key_count):
+    key_index = jnp.arange(key_count, dtype=jnp.int32)[None, None, None, :]
+    first = (query_index[None, :] - query_pos)[:, :, None, None]
+    return (key_index >= first) & (key_index <= query_index[None, :, None, None])
 
 
 def transposed_product(right_rows, pieces):
@@ -83,14 +83,18 @@
     return jnp.dot(left_rows, pieces, preferred_element_type=jnp.float32)
 
 
-def fold_grads(exchanged, pieces):
-    cuts = [member for member in exchanged]
-    return (
-        transposed_left(pieces[0], cuts[0]),
-        transposed_left(pieces[1], cuts[1]),
-        transposed_left(cuts[2], pieces[2]),
-        transposed_left(cuts[3], pieces[3]),
-    )
+def ctx_gather(rows):
+    return lax.all_gather(rows, "ctx", axis=0, tiled=True)
+
+
+def swap_blocks(blocks, axis_name):
+    return lax.all_to_all(blocks, axis_name, split_axis=0, concat_axis=0, tiled=True)
+
+
+def scatter_sum(partial, axis_name):
+    members = lax.axis_size(axis_name)
+    blocks = partial.astype(jnp.bfloat16).reshape(members, -1, partial.shape[-1])
+    return jnp.sum(swap_blocks(blocks, axis_name).astype(jnp.float32), axis=0)
 
 
 def attention_forward(queries, key_rows, value_rows, allowed, score_scale):
@@ -160,14 +164,52 @@
     scale_key,
     grad_output,
 ):
+    ctx_size = lax.axis_size("ctx")
+    fsdp_size = lax.axis_size("fsdp")
+    ctx_index = lax.axis_index("ctx")
     seq_count = block_input.shape[1]
     seq_rows = block_input.shape[2]
     row_count = seq_count * seq_rows
+    key_count = ctx_size * seq_rows
     head_total = HEADS * HEAD_DIM
     score_scale = HEAD_DIM ** (-0.5)
-    qkv_full, out_full = (
-        lax.all_gather(qkv_weight, "fsdp", axis=0, tiled=True),
-        lax.all_gather(out_weight, "fsdp", axis=0, tiled=True),
+    part = FF // ctx_size
+    piece = part // fsdp_size
+    qkv_rows = qkv_weight.shape[0] // ctx_size
+    out_rows = out_weight.shape[0] // ctx_size
+    qkv_full = lax.all_gather(
+        lax.dynamic_slice_in_dim(qkv_weight, ctx_index * qkv_rows, qkv_rows, 0),
+        ("fsdp", "ctx"),
+        axis=0,
+        tiled=True,
+    )
+    out_full = lax.all_gather(
+        lax.dynamic_slice_in_dim(out_weight, ctx_index * out_rows, out_rows, 0),
+        ("fsdp", "ctx"),
+        axis=0,
+        tiled=True,
+    )
+    down_piece = lax.ppermute(
+        lax.dynamic_slice_in_dim(down_weight, ctx_index * piece, piece, 0),
+        ("ctx", "fsdp"),
+        [
+            (c * fsdp_size + f, (c + ctx_size * f))
+            for c in range(ctx_size)
+            for f in range(fsdp_size)
+        ],
+    )
+    down_part = lax.all_gather(down_piece, "fsdp", axis=0, tiled=True)
+    gate_part_w = lax.all_gather(
+        lax.dynamic_slice_in_dim(gate_up_weight, ctx_index * part, part, 1),
+        "fsdp",
+        axis=0,
+        tiled=True,
+    )
+    up_part_w = lax.all_gather(
+        lax.dynamic_slice_in_dim(gate_up_weight, FF + ctx_index * part, part, 1),
+        "fsdp",
+        axis=0,
+        tiled=True,
     )
     resid_in = block_input.reshape(row_count, D).astype(jnp.float32)
     scale_one = rms_scale(resid_in)
@@ -179,21 +221,18 @@
     query_scale = rms_scale(query_raw)
     key_scale = rms_scale(key_raw)
     local_pos = positions.reshape(seq_count, seq_rows)
-    local_doc = doc_ids.reshape(seq_count, seq_rows)
     cosine, sine_part = rope_tables(local_pos.reshape(row_count))
     queries = rotate(
         query_raw * query_scale * scale_query, cosine[:, None, :], sine_part[:, None, :]
     ).astype(jnp.bfloat16)
     key_rows = rotate(key_raw * key_scale * scale_key, cosine, sine_part).astype(jnp.bfloat16)
-    key_all, value_all, pos_all, doc_all = (
-        lax.all_gather(key_rows.reshape(seq_count, seq_rows, HEAD_DIM), "ctx", axis=1, tiled=True),
-        lax.all_gather(
-            value_rows.reshape(seq_count, seq_rows, HEAD_DIM), "ctx", axis=1, tiled=True
-        ),
-        lax.all_gather(local_pos, "ctx", axis=1, tiled=True),
-        lax.all_gather(local_doc, "ctx", axis=1, tiled=True),
-    )
-    allowed = allowed_mask(local_pos, local_doc, pos_all, doc_all)
+    key_value = ctx_gather(jnp.concatenate([key_rows, value_rows], axis=1))
+    key_value = key_value.reshape(ctx_size, seq_count, seq_rows, 2 * HEAD_DIM)
+    key_value = key_value.transpose(1, 0, 2, 3).reshape(seq_count, key_count, 2 * HEAD_DIM)
+    key_all = key_value[:, :, :HEAD_DIM]
+    value_all = key_value[:, :, HEAD_DIM:]
+    query_index = ctx_index * seq_rows + jnp.arange(seq_rows, dtype=jnp.int32)
+    allowed = allowed_mask(local_pos, query_index, key_count)
     query_blocks = queries.reshape(seq_count, seq_rows, HEADS, HEAD_DIM)
     attended, log_total = attention_forward(query_blocks, key_all, value_all, allowed, score_scale)
     attended_low = attended.reshape(row_count, head_total).astype(jnp.bfloat16)
@@ -202,24 +241,44 @@
     middle = resid_in + projected * scale_two * scale_attn_out
     scale_three = rms_scale(middle)
     ff_input = (middle * scale_three * scale_ff_in).astype(jnp.bfloat16)
-    gate_up = add_product(ff_input, lax.all_gather(gate_up_weight, "fsdp", axis=0, tiled=True))
-    gate_part = gate_up[:, :FF]
-    up_part = gate_up[:, FF:]
+    ff_all = ctx_gather(ff_input)
+    gate_part = add_product(ff_all, gate_part_w)
+    up_part = add_product(ff_all, up_part_w)
     gelu_value, gelu_slope = gelu_parts(gate_part)
     activation = (gelu_value * up_part).astype(jnp.bfloat16)
-    down_out = add_product(activation, lax.all_gather(down_weight, "fsdp", axis=0, tiled=True))
+    down_out = scatter_sum(add_product(activation, down_part), "ctx")
     scale_four = rms_scale(down_out)
     block_output = (middle + down_out * scale_four * scale_ff_out).astype(jnp.bfloat16)
     cotangent = grad_output.reshape(row_count, D).astype(jnp.float32)
     ff_out_grad = jnp.sum(cotangent * down_out * scale_four, axis=0)
     down_cot = norm_back(down_out, scale_four, scale_ff_out, cotangent).astype(jnp.bfloat16)
-    act_cot = transposed_product(down_cot, lax.all_gather(down_weight, "fsdp", axis=0, tiled=True))
-    gate_up_cot = jnp.concatenate(
-        [act_cot * up_part * gelu_slope, act_cot * gelu_value], axis=1
-    ).astype(jnp.bfloat16)
-    ff_input_cot = transposed_product(
-        gate_up_cot, lax.all_gather(gate_up_weight, "fsdp", axis=0, tiled=True)
-    )
+    down_cot_all = ctx_gather(down_cot)
+    act_cot = transposed_product(down_cot_all, down_part)
+    gate_cot = (act_cot * up_part * gelu_slope).astype(jnp.bfloat16)
+    up_cot = (act_cot * gelu_value).astype(jnp.bfloat16)
+    ff_input_cot = scatter_sum(
+        transposed_product(gate_cot, gate_part_w) + transposed_product(up_cot, up_part_w), "ctx"
+    )
+    gate_up_sum = scatter_sum(
+        jnp.concatenate(
+            [transposed_left(gate_cot, ff_all), transposed_left(up_cot, ff_all)], axis=0
+        ),
+        "fsdp",
+    )
+    down_grad = scatter_sum(transposed_left(activation, down_cot_all), "fsdp")
+    half = fsdp_size // 2
+    gate_up_grad = lax.ppermute(
+        gate_up_sum,
+        ("ctx", "fsdp"),
+        [
+            (
+                c * fsdp_size + f,
+                half * c + f % half + (f // half) * (ctx_size * half),
+            )
+            for c in range(ctx_size)
+            for f in range(fsdp_size)
+        ],
+    ).T
     ff_in_grad = jnp.sum(ff_input_cot * middle * scale_three, axis=0)
     middle_cot = cotangent + norm_back(middle, scale_three, scale_ff_in, ff_input_cot)
     attn_out_grad = jnp.sum(middle_cot * projected * scale_two, axis=0)
@@ -235,14 +294,12 @@
         attended,
         attended_cot.reshape(seq_count, seq_rows, HEADS, HEAD_DIM),
     )
-    kv_local = lax.psum_scatter(
-        jnp.concatenate([key_cot, value_cot], axis=2).astype(jnp.bfloat16),
-        "ctx",
-        scatter_dimension=1,
-        tiled=True,
-    ).astype(jnp.float32)
-    key_cot_local = kv_local[:, :, :HEAD_DIM].reshape(row_count, HEAD_DIM)
-    value_cot_local = kv_local[:, :, HEAD_DIM:].reshape(row_count, HEAD_DIM)
+    kv_partial = jnp.concatenate([key_cot, value_cot], axis=2).reshape(
+        seq_count, ctx_size, seq_rows, 2 * HEAD_DIM
+    )
+    kv_local = scatter_sum(kv_partial.transpose(1, 0, 2, 3), "ctx")
+    key_cot_local = kv_local[:, :HEAD_DIM]
+    value_cot_local = kv_local[:, HEAD_DIM:]
     query_back = rotate_back(
         query_cot.reshape(row_count, HEADS, HEAD_DIM), cosine[:, None, :], sine_part[:, None, :]
     )
@@ -262,38 +319,28 @@
     attn_input_cot = transposed_product(qkv_cot, qkv_full)
     attn_in_grad = jnp.sum(attn_input_cot * resid_in * scale_one, axis=0)
     input_grad = middle_cot + norm_back(resid_in, scale_one, scale_attn_in, attn_input_cot)
-    gain_sums = lax.psum(
-        (attn_in_grad, attn_out_grad, ff_in_grad, ff_out_grad, query_gain_grad, key_gain_grad),
-        ("ctx", "fsdp"),
-    )
-    exchanged = (
-        lax.all_to_all(qkv_cot, ("ctx", "fsdp"), split_axis=1, concat_axis=0, tiled=True),
-        lax.all_to_all(gate_up_cot, ("ctx", "fsdp"), split_axis=1, concat_axis=0, tiled=True),
-        lax.all_to_all(attended_low, ("ctx", "fsdp"), split_axis=1, concat_axis=0, tiled=True),
-        lax.all_to_all(activation, ("ctx", "fsdp"), split_axis=1, concat_axis=0, tiled=True),
-    )
-    qkv_grad, gate_up_grad, out_grad, down_grad = fold_grads(
-        exchanged,
-        (
-            lax.all_gather(attn_input, ("ctx", "fsdp"), axis=0, tiled=True),
-            lax.all_gather(ff_input, ("ctx", "fsdp"), axis=0, tiled=True),
-            lax.all_gather(projected_cot, ("ctx", "fsdp"), axis=0, tiled=True),
-            lax.all_gather(down_cot, ("ctx", "fsdp"), axis=0, tiled=True),
-        ),
-    )
+    qkv_sum = scatter_sum(scatter_sum(transposed_left(qkv_cot, attn_input), "ctx"), "fsdp")
+    out_grad = scatter_sum(
+        scatter_sum(transposed_left(attended_low, projected_cot), "ctx"), "fsdp"
+    )
+    gains = jnp.concatenate(
+        [attn_in_grad, attn_out_grad, ff_in_grad, ff_out_grad, query_gain_grad, key_gain_grad]
+    )
+    gains = jnp.sum(lax.all_gather(gains, "ctx"), axis=0)
+    gains = jnp.sum(lax.all_gather(gains, "fsdp"), axis=0)
     return (
         block_output.reshape(1, seq_count, seq_rows, D),
         input_grad.reshape(1, seq_count, seq_rows, D),
-        qkv_grad,
+        qkv_sum.T,
         out_grad,
         gate_up_grad,
         down_grad,
-        gain_sums[0],
-        gain_sums[1],
-        gain_sums[2],
-        gain_sums[3],
-        gain_sums[4],
-        gain_sums[5],
+        gains[:D],
+        gains[D : 2 * D],
+        gains[2 * D : 3 * D],
+        gains[3 * D : 4 * D],
+        gains[4 * D : 4 * D + HEAD_DIM],
+        gains[4 * D + HEAD_DIM :],
     )
 
 

time: 2280 us -> 840 us (0.37)
  waiting for transfers between devices: 1840 us -> 374 us
  blocking collectives: 134 us -> 236 us
  matrix products: 136 us -> 70.6 us
  local copies, waits for them, and re-layouts: 73.5 us -> 36.1 us
  starting transfers between devices: 40.2 us -> 64.2 us
    all_gather x10 -> x5, waiting for transfers between devices: 1720 us -> 196 us  [the longest x1 68 us: on_device(): lax.all_gather(lax.dynamic_slice_in_dim(qkv_weight, ctx_index * qkv_rows,...]
    all_gather x2 -> x5, blocking collectives: 37.4 us -> 169 us  [the longest x1 41.8 us: on_device(): lax.all_gather(lax.dynamic_slice_in_dim(gate_up_weight, ctx_index * part,...]
    all_to_all x4 -> x8, waiting for transfers between devices: 0.01 us -> 118 us  [swap_blocks(): lax.all_to_all(blocks, axis_name, split_axis=0, concat_axis=0, tiled=True)]
    unnamed x12 -> x5, waiting for transfers between devices: 116 us -> 0.08 us
    psum x1 -> x0, blocking collectives: 96.3 us -> none  [on_device(): lax.psum((attn_in_grad, attn_out_grad, ff_in_grad, ff_out_grad, query_gai...]
    all_to_all x0 -> x1, blocking collectives: none -> 66.7 us  [swap_blocks(): lax.all_to_all(blocks, axis_name, split_axis=0, concat_axis=0, tiled=True)]
    ppermute x0 -> x2, waiting for transfers between devices: none -> 59.7 us  [the longest x1 59.7 us: on_device(): lax.ppermute(gate_up_sum, ('ctx', 'fsdp'), [(c * fsdp_size + f, half * c...]
    dot_general x4 -> x5, matrix products: 64.5 us -> 20.6 us  [transposed_left(): lax.dot_general(left_rows, right_rows, (((0,), (0,)), ((), ())), preferre...]
  transfers between devices with their start and end apart: 15 -> 15, of which waited for: 10 -> 12; matrix products, arithmetic and copies ran while one was open for 7% -> 10% of each run, Pallas kernels for 0% -> 0%
where the time goes in v1:
time: 840 us; the launch traced here: 828 us
  waiting for transfers between devices  374 us (45%)
  blocking collectives  236 us (28%)
  matrix products  70.6 us (8%)
  starting transfers between devices  64.2 us (8%)
  local copies, waits for them, and re-layouts  36.1 us (4%)
  other arithmetic  31.6 us (4%)
  between operations  15.2 us (2%)
    all_to_all x8, waiting for transfers between devices, swap_blocks(): lax.all_to_all(blocks, axis_name, split_axis=0, concat_axis=0, tiled=True)  118 us
    all_gather x1, waiting for transfers between devices, on_device(): lax.all_gather(lax.dynamic_slice_in_dim(qkv_weight, ctx_index * qkv_rows,...  68 us
    all_to_all x1, blocking collectives, swap_blocks(): lax.all_to_all(blocks, axis_name, split_axis=0, concat_axis=0, tiled=True)  66.7 us
    all_gather x3, waiting for transfers between devices, ctx_gather(): return lax.all_gather(rows, 'ctx', axis=0, tiled=True)  66.5 us
    all_gather x1, waiting for transfers between devices, on_device(): lax.all_gather(lax.dynamic_slice_in_dim(out_weight, ctx_index * out_rows,...  61.9 us
    ppermute x1, waiting for transfers between devices, on_device(): lax.ppermute(gate_up_sum, ('ctx', 'fsdp'), [(c * fsdp_size + f, half * c...  59.7 us
    all_to_all x8, starting transfers between devices, swap_blocks(): lax.all_to_all(blocks, axis_name, split_axis=0, concat_axis=0, tiled=True)  57.7 us
    all_gather x1, blocking collectives, on_device(): lax.all_gather(lax.dynamic_slice_in_dim(gate_up_weight, ctx_index * part,...  41.8 us
  transfers between devices with their start and end apart: 15, of which 12 were waited for; matrix products, arithmetic and copies ran while one was open for 10% of the time, Pallas kernels for 0%

profile of v1, /device:TPU:14, one launch (start us, length us, event | category | flops | bytes accessed | tf_op | source)
XLA Modules:
  0.0 828.1 jit_solution(11548138921891848561)
XLA Ops:
  12.1 68.0 %all-gather.18.cloned.1.call-done = bf16[128,9,1536]{2,1,0:T(8,128)(2,1)} async-done(((bf16[1,9,1536]{2,1,0:T(8,128)(2,1)}), bf16[128,9,1536]{2,1,0:T(8,128)(2,1)}) %all-gather.18.cloned.1.call-update) | async-done | bytes 3538960 | tf_op jit(solution)/shard_map/all_gather | solution.py:180
  80.1 7.5 reshape.355
  97.4 27.8 %all-gather.10.cloned.1.call-done = bf16[2048,512]{1,0:T(8,128)(2,1)} async-done(((bf16[128,512]{1,0:T(8,128)(2,1)}), bf16[2048,512]{1,0:T(8,128)(2,1)}) %all-gather.10.cloned.1.call-update) | async-done | bytes 2097168 | tf_op jit(solution)/shard_map/all_gather | solution.py:87
  131.0 61.9 %all-gather.12.cloned.1.call-done = bf16[1024,1152]{1,0:T(8,128)(2,1)} async-done(((bf16[8,1152]{1,0:T(8,128)(2,1)}), bf16[1024,1152]{1,0:T(8,128)(2,1)}) %all-gather.12.cloned.1.call-update) | async-done | bytes 2359312 | tf_op jit(solution)/shard_map/all_gather | solution.py:186
  202.5 41.8 %all_gather.40 = bf16[1152,432]{1,0:T(8,128)(2,1)} all-gather(bf16[144,432]{1,0:T(8,128)(2,1)S(1)} %get-tuple-element.27), channel_id=1, replica_groups=mesh['ctx'=16,'fsdp'=8] {'fsdp'}, dimensions={0}, use_global_device_ids=true | all-gather | bytes 1119744 | tf_op jit(solution)/shard_map/all_gather | solution.py:202
  244.3 40.7 %all_gather.41 = bf16[1152,432]{1,0:T(8,128)(2,1)} all-gather(bf16[144,432]{1,0:T(8,128)(2,1)S(1)} %get-tuple-element.28), channel_id=1, replica_groups=mesh['ctx'=16,'fsdp'=8] {'fsdp'}, dimensions={0}, use_global_device_ids=true | all-gather | bytes 1119744 | tf_op jit(solution)/shard_map/all_gather | solution.py:208
  285.0 38.3 %all-gather.3 = bf16[8,54,1152]{2,1,0:T(8,128)(2,1)S(1)} all-gather(bf16[1,54,1152]{2,1,0:T(8,128)(2,1)S(1)} %bitcast.171), channel_id=1, replica_groups=mesh['ctx'=16,'fsdp'=8] {'fsdp'}, dimensions={0}, use_global_device_ids=true | all-gather | bytes 1119744 | tf_op jit(solution)/shard_map/all_gather | solution.py:201
  324.5 5.3 fusion.77
  329.9 5.2 multiply_convert_fusion.1
  338.3 66.7 %all_to_all.45 = bf16[16,128,1152]{2,1,0:T(8,128)(2,1)S(1)} all-to-all(bf16[16,128,1152]{2,1,0:T(8,128)(2,1)S(1)} %bitcast.149), channel_id=1, replica_groups=mesh['ctx'=16,'fsdp'=8] {'ctx'}, dimensions={0} | all-to-all | bytes 9437184 | tf_op jit(solution)/shard_map/all_to_all | solution.py:91
  407.3 38.7 %all-gather.16.cloned.1.call-done = bf16[2048,1152]{1,0:T(8,128)(2,1)} async-done(((bf16[128,1152]{1,0:T(8,128)(2,1)}), bf16[2048,1152]{1,0:T(8,128)(2,1)}) %all-gather.16.cloned.1.call-update) | async-done | bytes 4718608 | tf_op jit(solution)/shard_map/all_gather | solution.py:87
  446.0 9.1 %multiply_convert_fusion = (bf16[2048,432]{0,1:T(8,128)(2,1)S(1)}, bf16[2048,432]{0,1:T(8,128)(2,1)S(1)}) fusion(f32[2048,432]{0,1:T(8,128)} %copy-done.68, f32[2048,432]{0,1:T(8,128)} %get-tuple-element.60, bf16[2048,1152]{1,0:T(8,128)(2,1)} %all-gather.16.cloned.1.call-done, bf16[432,1152]{1,0:T(8,128)(2,1)} %reshape.357), kind=kOutput, calls=%fused_computation.17 | convolution fusion | flops 2058780672 | bytes 16330752 | tf_op jit(solution)/shard_map/dot_general | solution.py:71
  462.9 6.3 all-to-all-start.1
  469.8 5.3 convolution_convert_fusion.3
  476.5 5.4 convolution_convert_fusion.4
  481.9 4.8 convolution_convert_fusion.5
  488.4 48.0 %all-to-all-done.1 = bf16[16,128,1152]{2,1,0:T(8,128)(2,1)} async-done(((bf16[16,128,1152]{2,1,0:T(8,128)(2,1)}), bf16[16,128,1152]{2,1,0:T(8,128)(2,1)}, u32[]{:S(2)}, u32[]{:S(2)}) %all-to-all-start.1) | async-done | bytes 4718624 | tf_op jit(solution)/shard_map/all_to_all | solution.py:91
  536.4 7.4 all-to-all-start.8
  547.6 10.4 %all-to-all-done.8 = bf16[8,54,1152]{2,1,0:T(8,128)(2,1)} async-done(((bf16[8,54,1152]{2,1,0:T(8,128)(2,1)}), bf16[8,54,1152]{2,1,0:T(8,128)(2,1)}, u32[]{:S(2)}, u32[]{:S(2)}) %all-to-all-start.8) | async-done | bytes 995360 | tf_op jit(solution)/shard_map/all_to_all | solution.py:91
  558.0 6.9 all-to-all-start.7
  581.9 7.2 all-to-all-done.7
  589.1 9.5 %all-to-all-start.2 = ((bf16[16,128,512]{2,1,0:T(8,128)(2,1)}), bf16[16,128,512]{2,1,0:T(8,128)(2,1)}, u32[]{:S(2)}, u32[]{:S(2)}) async-start(bf16[16,128,512]{2,1,0:T(8,128)(2,1)} %bitcast.146), calls=%async_computation.2 | async-start | bytes 4194304 | tf_op jit(solution)/shard_map/all_to_all | solution.py:91
  603.7 21.8 %all-to-all-done.2 = bf16[16,128,512]{2,1,0:T(8,128)(2,1)} async-done(((bf16[16,128,512]{2,1,0:T(8,128)(2,1)}), bf16[16,128,512]{2,1,0:T(8,128)(2,1)}, u32[]{:S(2)}, u32[]{:S(2)}) %all-to-all-start.2) | async-done | bytes 2097184 | tf_op jit(solution)/shard_map/all_to_all | solution.py:91
  625.5 7.4 all-to-all-start.5
  640.1 24.0 %all-to-all-done.5 = bf16[16,64,1152]{2,1,0:T(8,128)(2,1)} async-done(((bf16[16,64,1152]{2,1,0:T(8,128)(2,1)}), bf16[16,64,1152]{2,1,0:T(8,128)(2,1)}, u32[]{:S(2)}, u32[]{:S(2)}) %all-to-all-start.5) | async-done | bytes 2359328 | tf_op jit(solution)/shard_map/all_to_all | solution.py:91
  664.1 7.2 all-to-all-start.3
  678.6 59.7 %collective-permute-done.1 = f32[108,1152]{1,0:T(8,128)S(1)} collective-permute-done((f32[108,1152]{1,0:T(8,128)S(1)}, f32[108,1152]{1,0:T(8,128)S(1)}, u32[]{:S(2)}, u32[]{:S(2)}) %collective-permute-start.1) | collective-permute-done | bytes 497696 | tf_op jit(solution)/shard_map/ppermute | solution.py:270
  742.5 14.7 %all-gather = f32[81920]{0:T(1024)S(1)} all-gather(f32[5120]{0:T(1024)S(1)} %constant_dynamic-update-slice_fusion), channel_id=2, replica_groups=mesh['ctx'=16,'fsdp'=8] {'ctx'}, dimensions={0}, use_global_device_ids=true | all-gather | bytes 348160 | tf_op jit(solution)/shard_map/all_gather | solution.py:329
  757.4 33.8 %all-gather.1 = f32[40960]{0:T(1024)S(1)} all-gather(f32[5120]{0:T(1024)S(1)} %reduce_sum.326), channel_id=3, replica_groups=mesh['ctx'=16,'fsdp'=8] {'fsdp'}, dimensions={0}, use_global_device_ids=true | all-gather | bytes 184320 | tf_op jit(solution)/shard_map/all_gather | solution.py:330
  795.0 6.9 all-to-all-start.6
  807.5 6.1 all-to-all-start.4
  814.8 5.1 all-to-all-done.4
  (276 shorter events, 103.9 us)
Async XLA Ops:
  7.2 190.2 %copy-start = (bf16[864,1152]{1,0:T(8,128)(2,1)S(1)}, bf16[864,1152]{1,0:T(8,128)(2,1)}, u32[]{:S(2)}) copy-start(bf16[864,1152]{1,0:T(8,128)(2,1)} %param.19) | copy-start | bytes 5971972
  7.2 72.9 %all-gather.18.cloned.1.call-start = ((), (), s32[]{:S(2)}) async-start(), calls=%async_computation.13 | async-start | bytes 6340608 | tf_op jit(solution)/shard_map/all_gather | solution.py:180
  8.9 116.3 %all-gather.10.cloned.1.call-start = ((), (), s32[]{:S(2)}) async-start(), calls=%async_computation.9 | async-start | bytes 2228224 | tf_op jit(solution)/shard_map/all_gather | solution.py:87
  9.7 81.4 %copy-start.58 = (f32[128]{0:T(128)}, f32[128]{0:T(128)S(1)}, u32[]{:S(2)}) copy-start(f32[128]{0:T(128)S(1)} %convert_element_type.134) | copy-start | bytes 1540
  10.9 69.1 %copy-start.62 = (f32[128]{0:T(128)}, f32[128]{0:T(128)S(1)}, u32[]{:S(2)}) copy-start(f32[128]{0:T(128)S(1)} %rsqrt.56) | copy-start | bytes 1540
  11.0 80.2 %copy-start.60 = (f32[128]{0:T(128)}, f32[128]{0:T(128)S(1)}, u32[]{:S(2)}) copy-start(f32[128]{0:T(128)S(1)} %multiply_power_fusion) | copy-start | bytes 1540
  12.1 75.5 %copy-start.9 = (bf16[128,1152]{1,0:T(8,128)(2,1)}, bf16[128,1152]{1,0:T(8,128)(2,1)S(1)}, u32[]{:S(2)}) copy-start(bf16[128,1152]{1,0:T(8,128)(2,1)S(1)} %fusion.31) | copy-start | bytes 884740
  92.3 100.6 %all-gather.12.cloned.1.call-start = ((), (), s32[]{:S(2)}) async-start(), calls=%async_computation.10 | async-start | bytes 2377728 | tf_op jit(solution)/shard_map/all_gather | solution.py:186
  93.7 230.8 %all-gather.14.cloned.1.call-start = ((), (), s32[]{:S(2)}) async-start(), calls=%async_computation.11 | async-start | bytes 5013504 | tf_op jit(solution)/shard_map/all_gather | solution.py:87
  94.7 32.3 %copy-start.2 = (f32[128,1024]{1,0:T(8,128)}, f32[128,1024]{1,0:T(8,128)S(1)}, u32[]{:S(2)}) copy-start(f32[128,1024]{1,0:T(8,128)S(1)} %slice.85) | copy-start | bytes 1572868
  97.1 29.9 %copy-start.40 = (f32[128,4]{0,1:T(4,128)}, f32[128,4]{0,1:T(4,128)S(1)}, u32[]{:S(2)}) copy-start(f32[128,4]{0,1:T(4,128)S(1)} %add_rsqrt_fusion) | copy-start | bytes 6148
  97.3 29.8 %copy-start.31 = (pred[2,64,1024]{2,1,0:T(8,128)(4,1)S(1)}, pred[2,64,1024]{2,1,0:T(8,128)(4,1)}, u32[]{:S(2)}) copy-start(pred[2,64,1024]{2,1,0:T(8,128)(4,1)} %fusion.46) | copy-start | bytes 393220
  97.4 30.3 %copy-start.27 = (bf16[128,4,128]{2,0,1:T(8,128)(2,1)}, bf16[128,4,128]{2,0,1:T(8,128)(2,1)S(1)}, u32[]{:S(2)}) copy-start(bf16[128,4,128]{2,0,1:T(8,128)(2,1)S(1)} %get-tuple-element.33) | copy-start | bytes 393220
  97.4 30.3 %copy-start.29 = (bf16[128,4,128]{2,0,1:T(8,128)(2,1)}, bf16[128,4,128]{2,0,1:T(8,128)(2,1)S(1)}, u32[]{:S(2)}) copy-start(bf16[128,4,128]{2,0,1:T(8,128)(2,1)S(1)} %get-tuple-element.34) | copy-start | bytes 393220
  130.7 65.0 %copy-start.6 = (bf16[1,2,64,1152]{3,2,1,0:T(8,128)(2,1)S(1)}, bf16[1,2,64,1152]{3,2,1,0:T(8,128)(2,1)}, u32[]{:S(2)}) copy-start(bf16[1,2,64,1152]{3,2,1,0:T(8,128)(2,1)} %param.14) | copy-start | bytes 884740
  130.7 65.0 %copy-start.37 = (f32[1152]{0:T(1024)S(1)}, f32[1152]{0:T(1024)}, u32[]{:S(2)}) copy-start(f32[1152]{0:T(1024)} %param.21) | copy-start | bytes 13828
  131.0 64.2 %copy-start.11 = (bf16[16,8,4,256]{3,1,2,0:T(8,128)(2,1)}, bf16[16,8,4,256]{3,1,2,0:T(8,128)(2,1)S(1)}, u32[]{:S(2)}) copy-start(bf16[16,8,4,256]{3,1,2,0:T(8,128)(2,1)S(1)} %copy.114) | copy-start | bytes 786436
  131.0 65.5 %copy-start.36 = (f32[1152]{0:T(1024)S(1)}, f32[1152]{0:T(1024)}, u32[]{:S(2)}) copy-start(f32[1152]{0:T(1024)} %param.22) | copy-start | bytes 13828
  197.4 248.7 %all-gather.16.cloned.1.call-start = ((), (), s32[]{:S(2)}) async-start(), calls=%async_computation.12 | async-start | bytes 5013504 | tf_op jit(solution)/shard_map/all_gather | solution.py:87
  198.1 86.9 %collective-permute-start = (bf16[54,1152]{1,0:T(8,128)(2,1)}, bf16[54,1152]{1,0:T(8,128)(2,1)S(1)}, u32[]{:S(2)}, u32[]{:S(2)}) collective-permute-start(bf16[54,1152]{1,0:T(8,128)(2,1)} %constant_dynamic-slice_fusion), channel_id=1, source_target_pairs={{0,0},{1,16},{2,32},{3,48},{4,64},{5,80},{6,96},{7,112},{8,1},{9,1... | collective-permute-start | bytes 373256 | tf_op jit(solution)/shard_map/ppermute | solution.py:192
  462.9 73.4 %all-to-all-start.1 = ((bf16[16,128,1152]{2,1,0:T(8,128)(2,1)}), bf16[16,128,1152]{2,1,0:T(8,128)(2,1)}, u32[]{:S(2)}, u32[]{:S(2)}) async-start(bf16[16,128,1152]{2,1,0:T(8,128)(2,1)} %bitcast.148), calls=%async_computation.1 | async-start | bytes 9437184 | tf_op jit(solution)/shard_map/all_to_all | solution.py:91
  536.4 21.7 %all-to-all-start.8 = ((bf16[8,54,1152]{2,1,0:T(8,128)(2,1)}), bf16[8,54,1152]{2,1,0:T(8,128)(2,1)}, u32[]{:S(2)}, u32[]{:S(2)}) async-start(bf16[8,54,1152]{2,1,0:T(8,128)(2,1)} %reshape.349), calls=%async_computation.8 | async-start | bytes 2064384 | tf_op jit(solution)/shard_map/all_to_all | solution.py:91
  558.0 31.0 %all-to-all-start.7 = ((bf16[8,108,1152]{2,1,0:T(8,128)(2,1)}), bf16[8,108,1152]{2,1,0:T(8,128)(2,1)}, u32[]{:S(2)}, u32[]{:S(2)}) async-start(bf16[8,108,1152]{2,1,0:T(8,128)(2,1)} %convert_element_type.162), calls=%async_computation.7 | async-start | bytes 4128768 | tf_op jit(solution)/shard_map/all_to_all | solution.py:91
  589.1 36.5 %all-to-all-start.2 = ((bf16[16,128,512]{2,1,0:T(8,128)(2,1)}), bf16[16,128,512]{2,1,0:T(8,128)(2,1)}, u32[]{:S(2)}, u32[]{:S(2)}) async-start(bf16[16,128,512]{2,1,0:T(8,128)(2,1)} %bitcast.146), calls=%async_computation.2 | async-start | bytes 4194304 | tf_op jit(solution)/shard_map/all_to_all | solution.py:91
  625.5 38.6 %all-to-all-start.5 = ((bf16[16,64,1152]{2,1,0:T(8,128)(2,1)}), bf16[16,64,1152]{2,1,0:T(8,128)(2,1)}, u32[]{:S(2)}, u32[]{:S(2)}) async-start(bf16[16,64,1152]{2,1,0:T(8,128)(2,1)} %bitcast.143), calls=%async_computation.5 | async-start | bytes 4718592 | tf_op jit(solution)/shard_map/all_to_all | solution.py:91
  664.1 130.9 %all-to-all-start.3 = ((bf16[16,96,1152]{2,1,0:T(8,128)(2,1)}), bf16[16,96,1152]{2,1,0:T(8,128)(2,1)}, u32[]{:S(2)}, u32[]{:S(2)}) async-start(bf16[16,96,1152]{2,1,0:T(8,128)(2,1)} %bitcast.142), calls=%async_computation.3 | async-start | bytes 7077888 | tf_op jit(solution)/shard_map/all_to_all | solution.py:91
  671.4 67.7 %copy-start.21 = (bf16[128,1024]{1,0:T(8,128)(2,1)S(1)}, bf16[128,1024]{1,0:T(8,128)(2,1)}, u32[]{:S(2)}) copy-start(bf16[128,1024]{1,0:T(8,128)(2,1)} %copy-done.20) | copy-start | bytes 786436
  671.4 67.7 %copy-start.39 = (f32[1152]{0:T(1024)S(1)}, f32[1152]{0:T(1024)}, u32[]{:S(2)}) copy-start(f32[1152]{0:T(1024)} %param.20) | copy-start | bytes 13828
  671.4 67.7 %copy-start.63 = (f32[128]{0:T(128)S(1)}, f32[128]{0:T(128)}, u32[]{:S(2)}) copy-start(f32[128]{0:T(128)} %copy-done.62) | copy-start | bytes 1540
  673.4 64.9 %collective-permute-start.1 = (f32[108,1152]{1,0:T(8,128)S(1)}, f32[108,1152]{1,0:T(8,128)S(1)}, u32[]{:S(2)}, u32[]{:S(2)}) collective-permute-start(f32[108,1152]{1,0:T(8,128)S(1)} %convert_reduce_fusion.3), channel_id=1, source_target_pairs={{0,0},{1,1},{2,2},{3,3},{4,64},{5,65},{6,66},{7,67},{8,4},{9,5},{1... | collective-permute-start | bytes 1493000 | tf_op jit(solution)/shard_map/ppermute | solution.py:270
  795.0 12.4 %all-to-all-start.6 = ((bf16[8,8,1152]{2,1,0:T(8,128)(2,1)}), bf16[8,8,1152]{2,1,0:T(8,128)(2,1)S(1)}, u32[]{:S(2)}, u32[]{:S(2)}) async-start(bf16[8,8,1152]{2,1,0:T(8,128)(2,1)} %bitcast.32), calls=%async_computation.6 | async-start | bytes 294912 | tf_op jit(solution)/shard_map/all_to_all | solution.py:91
  807.5 12.4 %all-to-all-start.4 = ((bf16[8,12,1152]{2,1,0:T(8,128)(2,1)}), bf16[8,12,1152]{2,1,0:T(8,128)(2,1)S(1)}, u32[]{:S(2)}, u32[]{:S(2)}) async-start(bf16[8,12,1152]{2,1,0:T(8,128)(2,1)} %reshape.346), calls=%async_computation.4 | async-start | bytes 589824 | tf_op jit(solution)/shard_map/all_to_all | solution.py:91
  (53 other events, 252.8 us)
Sparse Core Ops, SparseCore 0:
  11.7 68.2 all-gather.17
  92.4 32.7 all-gather.9
  128.7 64.1 all-gather.11
  197.5 50.6 all-gather.13
  407.5 38.5 all-gather.15

commit v2 on v1

--- a/solution.py
+++ b/solution.py
@@ -1,7 +1,13 @@
+import functools
+
 import jax
 import jax.numpy as jnp
 from jax import lax
+from jax.experimental import pallas as pl
+from jax.experimental.pallas import tpu as pltpu
 from jax.sharding import PartitionSpec as P
+
+MESH = pl.DeviceIdType.MESH
 
 D = 1152
 FF = 6912
@@ -83,8 +89,236 @@
     return jnp.dot(left_rows, pieces, preferred_element_type=jnp.float32)
 
 
-def ctx_gather(rows):
-    return lax.all_gather(rows, "ctx", axis=0, tiled=True)
+def meet(axis_peers):
+    barrier = pltpu.get_barrier_semaphore()
+    for peer in axis_peers:
+        pl.semaphore_signal(barrier, inc=1, device_id=peer, device_id_type=MESH)
+    pl.semaphore_wait(barrier, len(axis_peers))
+
+
+def remote(source, target, send_sem, recv_sem, peer):
+    return pltpu.make_async_remote_copy(
+        src_ref=source,
+        dst_ref=target,
+        send_sem=send_sem,
+        recv_sem=recv_sem,
+        device_id=peer,
+        device_id_type=MESH,
+    )
+
+
+def gather_body(chips, x_ref, o_ref, send, recv, pass_send, pass_recv, own_sem):
+    me = lax.axis_index("ctx")
+    core = lax.rem(me, 2)
+    chip = me // 2
+    sibling = {"ctx": chip * 2 + 1 - core}
+    slots = [(chip ^ r) * 2 + core for r in range(chips)]
+    meet([sibling] + [{"ctx": slots[r]} for r in range(1, chips)])
+    own = pltpu.make_async_copy(x_ref, o_ref.at[me], own_sem)
+    own.start()
+    copies = []
+    for r in range(1, chips):
+        copies.append(remote(x_ref, o_ref.at[me], send.at[r], recv.at[r], {"ctx": slots[r]}))
+        copies[-1].start()
+    passed = [remote(x_ref, o_ref.at[me], pass_send.at[0], pass_recv.at[0], sibling)]
+    passed[0].start()
+    for r in range(1, chips):
+        copies[r - 1].wait_recv()
+        block = o_ref.at[slots[r]]
+        passed.append(remote(block, block, pass_send.at[r], pass_recv.at[r], sibling))
+        passed[-1].start()
+    own.wait()
+    for copy in copies:
+        copy.wait_send()
+    for copy in passed:
+        copy.wait()
+
+
+def ctx_gather(rows, collective_id):
+    members = lax.axis_size("ctx")
+    chips = members // 2
+    count, width = rows.shape
+    gathered = pl.pallas_call(
+        functools.partial(gather_body, chips),
+        out_shape=jax.ShapeDtypeStruct((members, count, width), rows.dtype),
+        in_specs=[pl.BlockSpec(memory_space=pltpu.VMEM)],
+        out_specs=pl.BlockSpec(memory_space=pl.ANY),
+        scratch_shapes=[pltpu.SemaphoreType.DMA((chips,))] * 4 + [pltpu.SemaphoreType.DMA],
+        compiler_params=pltpu.CompilerParams(collective_id=collective_id, has_side_effects=True),
+        name="ctx_gather",
+    )(rows)
+    return gathered.reshape(members * count, width)
+
+
+def scatter_body(
+    chips, rows, p_ref, o_ref, near, sums, far, near_send, near_recv, send, recv
+):
+    me = lax.axis_index("ctx")
+    core = lax.rem(me, 2)
+    chip = me // 2
+    sibling = {"ctx": chip * 2 + 1 - core}
+    slots = [(chip ^ r) * 2 + core for r in range(chips)]
+    meet([sibling] + [{"ctx": slots[r]} for r in range(1, chips)])
+    order = list(range(chips - 1, -1, -1))
+    steps = p_ref.shape[1] // rows
+    first = {}
+    for r in order:
+        block = p_ref.at[(chip ^ r) * 2 + 1 - core]
+        first[r] = remote(block, near.at[r], near_send.at[r], near_recv.at[r], sibling)
+        first[r].start()
+    second = {}
+    for r in order:
+        first[r].wait_recv()
+        if r:
+
+            @pl.loop(0, steps)
+            def _(i):
+                part = pl.ds(pl.multiple_of(i * rows, rows), rows)
+                total = p_ref[slots[r], part, :].astype(jnp.float32) + near[r, part, :].astype(
+                    jnp.float32
+                )
+                sums[r, part, :] = total.astype(jnp.bfloat16)
+
+            second[r] = remote(sums.at[r], far.at[r], send.at[r], recv.at[r], {"ctx": slots[r]})
+        if r + 1 < chips:
+            second[r + 1].start()
+    for r in order[:-1]:
+        second[r].wait_recv()
+
+    @pl.loop(0, steps)
+    def _(i):
+        part = pl.ds(pl.multiple_of(i * rows, rows), rows)
+        total = p_ref[slots[0], part, :].astype(jnp.float32) + near[0, part, :].astype(jnp.float32)
+        for r in order[:-1]:
+            total = total + far[r, part, :].astype(jnp.float32)
+        o_ref[part, :] = total
+
+    for r in order:
+        first[r].wait_send()
+    for r in order[:-1]:
+        second[r].wait_send()
+
+
+def ctx_scatter(partial, collective_id):
+    members = lax.axis_size("ctx")
+    chips = members // 2
+    width = partial.shape[-1]
+    blocks = partial.astype(jnp.bfloat16).reshape(members, -1, width)
+    count = blocks.shape[1]
+    buffer = pltpu.VMEM((chips, count, width), jnp.bfloat16)
+    return pl.pallas_call(
+        functools.partial(scatter_body, chips, 16),
+        out_shape=jax.ShapeDtypeStruct((count, width), jnp.float32),
+        in_specs=[pl.BlockSpec(memory_space=pltpu.VMEM)],
+        out_specs=pl.BlockSpec(memory_space=pltpu.VMEM),
+        scratch_shapes=[buffer] * 3 + [pltpu.SemaphoreType.DMA((chips,))] * 4,
+        compiler_params=pltpu.CompilerParams(collective_id=collective_id, has_side_effects=True),
+        name="ctx_scatter",
+    )(blocks)
+
+
+def weight_body(members, x_ref, o_ref, send, recv, pass_send, pass_recv, own_sem):
+    ctx = lax.axis_index("ctx")
+    core = lax.rem(ctx, 2)
+    me = lax.axis_index("fsdp")
+    sibling = {"ctx": (ctx // 2) * 2 + 1 - core}
+    meet([sibling] + [{"fsdp": me ^ r} for r in range(1, members)])
+    own = pltpu.make_async_copy(x_ref, o_ref.at[me], own_sem)
+    own.start()
+    copies = []
+    for r in range(1, members):
+        copies.append(
+            remote(
+                x_ref.at[core], o_ref.at[me, core], send.at[r], recv.at[r], {"fsdp": me ^ r}
+            )
+        )
+        copies[-1].start()
+    passed = []
+    for r in range(1, members):
+        copies[r - 1].wait_recv()
+        block = o_ref.at[me ^ r, core]
+        passed.append(remote(block, block, pass_send.at[r], pass_recv.at[r], sibling))
+        passed[-1].start()
+    own.wait()
+    for copy in copies:
+        copy.wait_send()
+    for copy in passed:
+        copy.wait()
+
+
+def weight_gather(shard, collective_id):
+    members = lax.axis_size("fsdp")
+    rows, width = shard.shape
+    halves = shard.reshape(2, rows // 2, width)
+    gathered = pl.pallas_call(
+        functools.partial(weight_body, members),
+        out_shape=jax.ShapeDtypeStruct((members,) + halves.shape, shard.dtype),
+        in_specs=[pl.BlockSpec(memory_space=pltpu.VMEM)],
+        out_specs=pl.BlockSpec(memory_space=pl.ANY),
+        scratch_shapes=[pltpu.SemaphoreType.DMA((members,))] * 4 + [pltpu.SemaphoreType.DMA],
+        compiler_params=pltpu.CompilerParams(collective_id=collective_id, has_side_effects=True),
+        name="weight_gather",
+    )(halves)
+    return gathered.reshape(members * rows, width)
+
+
+def gain_body(ctx_size, fsdp_size, x_ref, o_ref, held, subtotal, others, send, recv, send2, recv2):
+    ctx = lax.axis_index("ctx")
+    fsdp = lax.axis_index("fsdp")
+    ctx_peers = [{"ctx": ctx ^ r} for r in range(1, ctx_size)]
+    fsdp_peers = [{"fsdp": fsdp ^ r} for r in range(1, fsdp_size)]
+    meet(ctx_peers + fsdp_peers)
+    held[ctx] = x_ref[...]
+    copies = []
+    for r in range(1, ctx_size):
+        copies.append(remote(x_ref, held.at[ctx], send.at[r], recv.at[r], ctx_peers[r - 1]))
+        copies[-1].start()
+    for copy in copies:
+        copy.wait()
+    total = held[0]
+    for i in range(1, ctx_size):
+        total = total + held[i]
+    subtotal[...] = total
+    others[fsdp] = total
+    copies = []
+    for r in range(1, fsdp_size):
+        copies.append(
+            remote(subtotal, others.at[fsdp], send2.at[r], recv2.at[r], fsdp_peers[r - 1])
+        )
+        copies[-1].start()
+    for copy in copies:
+        copy.wait()
+    total = others[0]
+    for i in range(1, fsdp_size):
+        total = total + others[i]
+    o_ref[...] = total
+
+
+def gain_sum(vector, collective_id):
+    ctx_size = lax.axis_size("ctx")
+    fsdp_size = lax.axis_size("fsdp")
+    rows = vector.reshape(-1, 128)
+    return pl.pallas_call(
+        functools.partial(gain_body, ctx_size, fsdp_size),
+        out_shape=jax.ShapeDtypeStruct(rows.shape, jnp.float32),
+        in_specs=[pl.BlockSpec(memory_space=pltpu.VMEM)],
+        out_specs=pl.BlockSpec(memory_space=pltpu.VMEM),
+        scratch_shapes=[
+            pltpu.VMEM((ctx_size,) + rows.shape, jnp.float32),
+            pltpu.VMEM(rows.shape, jnp.float32),
+            pltpu.VMEM((fsdp_size,) + rows.shape, jnp.float32),
+        ]
+        + [pltpu.SemaphoreType.DMA((ctx_size,))] * 2
+        + [pltpu.SemaphoreType.DMA((fsdp_size,))] * 2,
+        compiler_params=pltpu.CompilerParams(collective_id=collective_id, has_side_effects=True),
+        name="gain_sum",
+    )(rows).reshape(-1)
+
+
+def spread(shard, axis_name):
+    members = lax.axis_size(axis_name)
+    copies = jnp.broadcast_to(shard[None], (members,) + shard.shape)
+    return swap_blocks(copies, axis_name).reshape(members * shard.shape[0], shard.shape[1])
 
 
 def swap_blocks(blocks, axis_name):
@@ -175,20 +409,8 @@
     score_scale = HEAD_DIM ** (-0.5)
     part = FF // ctx_size
     piece = part // fsdp_size
-    qkv_rows = qkv_weight.shape[0] // ctx_size
-    out_rows = out_weight.shape[0] // ctx_size
-    qkv_full = lax.all_gather(
-        lax.dynamic_slice_in_dim(qkv_weight, ctx_index * qkv_rows, qkv_rows, 0),
-        ("fsdp", "ctx"),
-        axis=0,
-        tiled=True,
-    )
-    out_full = lax.all_gather(
-        lax.dynamic_slice_in_dim(out_weight, ctx_index * out_rows, out_rows, 0),
-        ("fsdp", "ctx"),
-        axis=0,
-        tiled=True,
-    )
+    qkv_full = weight_gather(qkv_weight, 1)
+    out_full = weight_gather(out_weight, 2)
     down_piece = lax.ppermute(
         lax.dynamic_slice_in_dim(down_weight, ctx_index * piece, piece, 0),
         ("ctx", "fsdp"),
@@ -198,18 +420,12 @@
             for f in range(fsdp_size)
         ],
     )
-    down_part = lax.all_gather(down_piece, "fsdp", axis=0, tiled=True)
-    gate_part_w = lax.all_gather(
-        lax.dynamic_slice_in_dim(gate_up_weight, ctx_index * part, part, 1),
-        "fsdp",
-        axis=0,
-        tiled=True,
-    )
-    up_part_w = lax.all_gather(
-        lax.dynamic_slice_in_dim(gate_up_weight, FF + ctx_index * part, part, 1),
-        "fsdp",
-        axis=0,
-        tiled=True,
+    down_part = spread(down_piece, "fsdp")
+    gate_part_w = spread(
+        lax.dynamic_slice_in_dim(gate_up_weight, ctx_index * part, part, 1), "fsdp"
+    )
+    up_part_w = spread(
+        lax.dynamic_slice_in_dim(gate_up_weight, FF + ctx_index * part, part, 1), "fsdp"
     )
     resid_in = block_input.reshape(row_count, D).astype(jnp.float32)
     scale_one = rms_scale(resid_in)
@@ -226,7 +442,7 @@
         query_raw * query_scale * scale_query, cosine[:, None, :], sine_part[:, None, :]
     ).astype(jnp.bfloat16)
     key_rows = rotate(key_raw * key_scale * scale_key, cosine, sine_part).astype(jnp.bfloat16)
-    key_value = ctx_gather(jnp.concatenate([key_rows, value_rows], axis=1))
+    key_value = ctx_gather(jnp.concatenate([key_rows, value_rows], axis=1), 3)
     key_value = key_value.reshape(ctx_size, seq_count, seq_rows, 2 * HEAD_DIM)
     key_value = key_value.transpose(1, 0, 2, 3).reshape(seq_count, key_count, 2 * HEAD_DIM)
     key_all = key_value[:, :, :HEAD_DIM]
@@ -241,23 +457,23 @@
     middle = resid_in + projected * scale_two * scale_attn_out
     scale_three = rms_scale(middle)
     ff_input = (middle * scale_three * scale_ff_in).astype(jnp.bfloat16)
-    ff_all = ctx_gather(ff_input)
+    ff_all = ctx_gather(ff_input, 4)
     gate_part = add_product(ff_all, gate_part_w)
     up_part = add_product(ff_all, up_part_w)
     gelu_value, gelu_slope = gelu_parts(gate_part)
     activation = (gelu_value * up_part).astype(jnp.bfloat16)
-    down_out = scatter_sum(add_product(activation, down_part), "ctx")
+    down_out = ctx_scatter(add_product(activation, down_part), 6)
     scale_four = rms_scale(down_out)
     block_output = (middle + down_out * scale_four * scale_ff_out).astype(jnp.bfloat16)
     cotangent = grad_output.reshape(row_count, D).astype(jnp.float32)
     ff_out_grad = jnp.sum(cotangent * down_out * scale_four, axis=0)
     down_cot = norm_back(down_out, scale_four, scale_ff_out, cotangent).astype(jnp.bfloat16)
-    down_cot_all = ctx_gather(down_cot)
+    down_cot_all = ctx_gather(down_cot, 5)
     act_cot = transposed_product(down_cot_all, down_part)
     gate_cot = (act_cot * up_part * gelu_slope).astype(jnp.bfloat16)
     up_cot = (act_cot * gelu_value).astype(jnp.bfloat16)
-    ff_input_cot = scatter_sum(
-        transposed_product(gate_cot, gate_part_w) + transposed_product(up_cot, up_part_w), "ctx"
+    ff_input_cot = ctx_scatter(
+        transposed_product(gate_cot, gate_part_w) + transposed_product(up_cot, up_part_w), 7
     )
     gate_up_sum = scatter_sum(
         jnp.concatenate(
@@ -297,7 +513,7 @@
     kv_partial = jnp.concatenate([key_cot, value_cot], axis=2).reshape(
         seq_count, ctx_size, seq_rows, 2 * HEAD_DIM
     )
-    kv_local = scatter_sum(kv_partial.transpose(1, 0, 2, 3), "ctx")
+    kv_local = ctx_scatter(kv_partial.transpose(1, 0, 2, 3), 8)
     key_cot_local = kv_local[:, :HEAD_DIM]
     value_cot_local = kv_local[:, HEAD_DIM:]
     query_back = rotate_back(
@@ -319,15 +535,14 @@
     attn_input_cot = transposed_product(qkv_cot, qkv_full)
     attn_in_grad = jnp.sum(attn_input_cot * resid_in * scale_one, axis=0)
     input_grad = middle_cot + norm_back(resid_in, scale_one, scale_attn_in, attn_input_cot)
-    qkv_sum = scatter_sum(scatter_sum(transposed_left(qkv_cot, attn_input), "ctx"), "fsdp")
+    qkv_sum = scatter_sum(ctx_scatter(transposed_left(qkv_cot, attn_input), 9), "fsdp")
     out_grad = scatter_sum(
-        scatter_sum(transposed_left(attended_low, projected_cot), "ctx"), "fsdp"
+        ctx_scatter(transposed_left(attended_low, projected_cot), 10), "fsdp"
     )
     gains = jnp.concatenate(
         [attn_in_grad, attn_out_grad, ff_in_grad, ff_out_grad, query_gain_grad, key_gain_grad]
     )
-    gains = jnp.sum(lax.all_gather(gains, "ctx"), axis=0)
-    gains = jnp.sum(lax.all_gather(gains, "fsdp"), axis=0)
+    gains = gain_sum(gains, 11)
     return (
         block_output.reshape(1, seq_count, seq_rows, D),
         input_grad.reshape(1, seq_count, seq_rows, D),

time: 840 us -> 607 us (0.72)
  Pallas kernels: 0 us -> 360 us
  waiting for transfers between devices: 374 us -> 30.8 us
  blocking collectives: 236 us -> 0 us
  between operations: 15.2 us -> 2.1 us
    pallas_call x0 -> x11, Pallas kernels: none -> 360 us  [the longest x5 162 us: ctx_scatter(): pl.pallas_call(functools.partial(scatter_body, chips, 16), out_shape=jax....]
    all_gather x5 -> x0, waiting for transfers between devices: 196 us -> none  [the longest x1 68 us: on_device(): lax.all_gather(lax.dynamic_slice_in_dim(qkv_weight, ctx_index * qkv_rows,...]
    all_gather x5 -> x0, blocking collectives: 169 us -> none  [the longest x1 41.8 us: on_device(): lax.all_gather(lax.dynamic_slice_in_dim(gate_up_weight, ctx_index * part,...]
    all_to_all x8 -> x7, waiting for transfers between devices: 118 us -> 9.78 us  [swap_blocks(): lax.all_to_all(blocks, axis_name, split_axis=0, concat_axis=0, tiled=True)]
    all_to_all x1 -> x0, blocking collectives: 66.7 us -> none  [swap_blocks(): lax.all_to_all(blocks, axis_name, split_axis=0, concat_axis=0, tiled=True)]
    ppermute x1, waiting for transfers between devices: 59.7 us -> 21 us  [on_device(): lax.ppermute(gate_up_sum, ('ctx', 'fsdp'), [(c * fsdp_size + f, half * c...]
    reduce_sum x9 -> x4, other arithmetic: 16.4 us -> 5.77 us  [scatter_sum(): return jnp.sum(swap_blocks(blocks, axis_name).astype(jnp.float32), axis=0)]
    all_to_all x8 -> x7, starting transfers between devices: 57.7 us -> 51.8 us  [swap_blocks(): lax.all_to_all(blocks, axis_name, split_axis=0, concat_axis=0, tiled=True)]
  transfers between devices with their start and end apart: 15 -> 9, of which waited for: 12 -> 3; matrix products, arithmetic and copies ran while one was open for 10% -> 11% of each run, Pallas kernels for 0% -> 31%
where the time goes in v2:
time: 607 us; the launch traced here: 598 us
  Pallas kernels  360 us (59%)
  matrix products  74.5 us (12%)
  starting transfers between devices  56.9 us (9%)
  local copies, waits for them, and re-layouts  38.9 us (6%)
  other arithmetic  35 us (6%)
  waiting for transfers between devices  30.8 us (5%)
    pallas_call x5, Pallas kernels, ctx_scatter(): pl.pallas_call(functools.partial(scatter_body, chips, 16), out_shape=jax....  162 us
    pallas_call x3, Pallas kernels, ctx_gather(): pl.pallas_call(functools.partial(gather_body, chips), out_shape=jax.Shape...  107 us
    pallas_call x2, Pallas kernels, weight_gather(): pl.pallas_call(functools.partial(weight_body, members), out_shape=jax.Sha...  63.7 us
    all_to_all x7, starting transfers between devices, swap_blocks(): lax.all_to_all(blocks, axis_name, split_axis=0, concat_axis=0, tiled=True)  51.8 us
    pallas_call x1, Pallas kernels, gain_sum(): pl.pallas_call(functools.partial(gain_body, ctx_size, fsdp_size), out_sha...  27.3 us
    dot_general x5, matrix products, transposed_product(): lax.dot_general(right_rows, pieces, (((1,), (1,)), ((), ())), preferred_e...  23.6 us
    ppermute x1, waiting for transfers between devices, on_device(): lax.ppermute(gate_up_sum, ('ctx', 'fsdp'), [(c * fsdp_size + f, half * c...  21 us
    dot_general x3, matrix products, add_product(): return jnp.dot(left_rows, pieces, preferred_element_type=jnp.float32)  20.6 us
  transfers between devices with their start and end apart: 9, of which 3 were waited for; matrix products, arithmetic and copies ran while one was open for 11% of the time, Pallas kernels for 31%

profile of v2, /device:TPU:14, one launch (start us, length us, event | category | flops | bytes accessed | tf_op | source)
XLA Modules:
  0.0 598.1 jit_solution(1195685576885051940)
XLA Ops:
  2.9 3.2 collective-permute-start
  9.2 9.6 %all-to-all-start = ((bf16[8,144,432]{2,1,0:T(8,128)(2,1)}), bf16[8,144,432]{2,1,0:T(8,128)(2,1)}, u32[]{:S(2)}, u32[]{:S(2)}) async-start(bf16[8,144,432]{2,1,0:T(8,128)(2,1)} %broadcast_in_dim.27), calls=%async_computation | async-start | bytes 2359296 | tf_op jit(solution)/shard_map/all_to_all | solution.py:325
  19.1 40.7 %weight_gather.2 = bf16[8,2,72,1536]{3,2,1,0:T(8,128)(2,1)} custom-call(bf16[2,72,1536]{2,1,0:T(8,128)(2,1)} %bitcast.196), custom_call_target="tpu_custom_call" | custom-call | tf_op jit(solution)/shard_map/weight_gather/pallas_call | solution.py:253
  64.7 24.0 %ctx_gather.3 = bf16[16,128,512]{2,1,0:T(8,128)(2,1)} custom-call(bf16[128,512]{1,0:T(8,128)(2,1)} %pad_maximum_fusion.7.x_ref), custom_call_target="tpu_custom_call" | custom-call | tf_op jit(solution)/shard_map/ctx_gather/pallas_call | solution.py:141
  96.4 23.0 %weight_gather.3 = bf16[8,2,64,1152]{3,2,1,0:T(8,128)(2,1)} custom-call(bf16[2,64,1152]{2,1,0:T(8,128)(2,1)} %bitcast.198), custom_call_target="tpu_custom_call" | custom-call | tf_op jit(solution)/shard_map/weight_gather/pallas_call | solution.py:253
  125.3 7.5 %all-to-all-start.1 = ((bf16[8,144,432]{2,1,0:T(8,128)(2,1)}), bf16[8,144,432]{2,1,0:T(8,128)(2,1)}, u32[]{:S(2)}, u32[]{:S(2)}) async-start(bf16[8,144,432]{2,1,0:T(8,128)(2,1)} %broadcast_in_dim.28), calls=%async_computation.1 | async-start | bytes 2359296 | tf_op jit(solution)/shard_map/all_to_all | solution.py:325
  134.8 41.3 %ctx_gather.4 = bf16[16,128,1152]{2,1,0:T(8,128)(2,1)} custom-call(bf16[128,1152]{1,0:T(8,128)(2,1)} %multiply_convert_fusion.4.x_ref), custom_call_target="tpu_custom_call" | custom-call | tf_op jit(solution)/shard_map/ctx_gather/pallas_call | solution.py:141
  179.3 7.4 %all-to-all-start.2 = ((bf16[8,54,1152]{2,1,0:T(8,128)(2,1)}), bf16[8,54,1152]{2,1,0:T(8,128)(2,1)}, u32[]{:S(2)}, u32[]{:S(2)}) async-start(bf16[8,54,1152]{2,1,0:T(8,128)(2,1)} %broadcast_in_dim.29), calls=%async_computation.2 | async-start | bytes 2064384 | tf_op jit(solution)/shard_map/all_to_all | solution.py:325
  186.7 5.3 fusion.77
  193.7 8.5 %multiply_convert_fusion.1 = (bf16[2048,432]{0,1:T(8,128)(2,1)}, f32[2048,432]{0,1:T(8,128)}) fusion(f32[2048,432]{0,1:T(8,128)S(1)} %fusion.77, bf16[2048,1152]{1,0:T(8,128)(2,1)} %bitcast.170, bf16[1152,432]{1,0:T(8,128)(2,1)} %bitcast.18), kind=kOutput, calls=%fused_computation.15 | convolution fusion | flops 2047279104 | bytes 14561280 | tf_op jit(solution)/shard_map/dot_general | solution.py:89
  204.7 6.8 %convolution_convert_fusion = bf16[2048,1152]{1,0:T(8,128)(2,1)} fusion(bf16[2048,432]{0,1:T(8,128)(2,1)} %get-tuple-element.60, bf16[432,1152]{1,0:T(8,128)(2,1)} %reshape.370), kind=kOutput, calls=%fused_computation.1 | convolution fusion | flops 2040791040 | bytes 7483392 | tf_op jit(solution)/shard_map/dot_general | solution.py:89
  211.5 41.7 %ctx_scatter.5 = f32[128,1152]{1,0:T(8,128)} custom-call(bf16[16,128,1152]{2,1,0:T(8,128)(2,1)} %bitcast.176), custom_call_target="tpu_custom_call" | custom-call | tf_op jit(solution)/shard_map/ctx_scatter/pallas_call | solution.py:209
  258.7 41.4 %ctx_gather.5 = bf16[16,128,1152]{2,1,0:T(8,128)(2,1)} custom-call(bf16[128,1152]{1,0:T(8,128)(2,1)} %get-tuple-element.35.x_ref), custom_call_target="tpu_custom_call" | custom-call | tf_op jit(solution)/shard_map/ctx_gather/pallas_call | solution.py:141
  300.1 9.0 %multiply_convert_fusion = (bf16[2048,432]{0,1:T(8,128)(2,1)S(1)}, bf16[2048,432]{0,1:T(8,128)(2,1)S(1)}) fusion(f32[2048,432]{0,1:T(8,128)} %copy-done.65, f32[2048,432]{0,1:T(8,128)} %get-tuple-element.61, bf16[2048,1152]{1,0:T(8,128)(2,1)} %bitcast.167, bf16[432,1152]{1,0:T(8,128)(2,1)} %reshape.370), kind=kOutput, calls=%fused_computation.14 | convolution fusion | flops 2058780672 | bytes 16330752 | tf_op jit(solution)/shard_map/dot_general | solution.py:77
  309.1 5.9 convolution_convert_fusion.5
  315.0 4.3 fusion.78
  319.4 3.5 convolution_convert_fusion.4
  322.8 6.2 %add_convert_fusion = bf16[2048,1152]{1,0:T(8,128)(2,1)} fusion(f32[2048,1152]{1,0:T(8,128)S(1)} %fusion.78, bf16[2048,432]{0,1:T(8,128)(2,1)S(1)} %get-tuple-element.25, bf16[1152,432]{1,0:T(8,128)(2,1)} %bitcast.18), kind=kOutput, calls=%fused_computation | convolution fusion | flops 2043150336 | bytes 16920576 | tf_op jit(solution)/shard_map/dot_general | solution.py:77
  329.0 42.2 %ctx_scatter.6 = f32[128,1152]{1,0:T(8,128)} custom-call(bf16[16,128,1152]{2,1,0:T(8,128)(2,1)} %bitcast.175), custom_call_target="tpu_custom_call" | custom-call | tf_op jit(solution)/shard_map/ctx_scatter/pallas_call | solution.py:209
  389.5 21.6 %ctx_scatter.7 = f32[128,512]{1,0:T(8,128)} custom-call(bf16[16,128,512]{2,1,0:T(8,128)(2,1)} %bitcast.166), custom_call_target="tpu_custom_call" | custom-call | tf_op jit(solution)/shard_map/ctx_scatter/pallas_call | solution.py:209
  421.9 25.0 %ctx_scatter.9 = f32[64,1152]{1,0:T(8,128)} custom-call(bf16[16,64,1152]{2,1,0:T(8,128)(2,1)} %bitcast.161), custom_call_target="tpu_custom_call" | custom-call | tf_op jit(solution)/shard_map/ctx_scatter/pallas_call | solution.py:209
  448.6 7.5 %all-to-all-start.4 = ((bf16[8,8,1152]{2,1,0:T(8,128)(2,1)}), bf16[8,8,1152]{2,1,0:T(8,128)(2,1)}, u32[]{:S(2)}, u32[]{:S(2)}) async-start(bf16[8,8,1152]{2,1,0:T(8,128)(2,1)} %convert_bitcast_fusion), calls=%async_computation.4 | async-start | bytes 294912 | tf_op jit(solution)/shard_map/all_to_all | solution.py:325
  458.0 3.2 fusion.41
  464.1 31.6 %ctx_scatter.8 = f32[96,1152]{1,0:T(8,128)} custom-call(bf16[16,96,1152]{2,1,0:T(8,128)(2,1)} %bitcast.160), custom_call_target="tpu_custom_call" | custom-call | tf_op jit(solution)/shard_map/ctx_scatter/pallas_call | solution.py:209
  497.6 7.2 %all-to-all-start.3 = ((bf16[8,12,1152]{2,1,0:T(8,128)(2,1)}), bf16[8,12,1152]{2,1,0:T(8,128)(2,1)S(1)}, u32[]{:S(2)}, u32[]{:S(2)}) async-start(bf16[8,12,1152]{2,1,0:T(8,128)(2,1)} %reshape.380), calls=%async_computation.3 | async-start | bytes 589824 | tf_op jit(solution)/shard_map/all_to_all | solution.py:325
  507.7 4.0 all-to-all-done.3
  511.8 6.9 %all-to-all-start.5 = ((bf16[8,108,1152]{2,1,0:T(8,128)(2,1)}), bf16[8,108,1152]{2,1,0:T(8,128)(2,1)}, u32[]{:S(2)}, u32[]{:S(2)}) async-start(bf16[8,108,1152]{2,1,0:T(8,128)(2,1)} %convert_element_type.158), calls=%async_computation.5 | async-start | bytes 4128768 | tf_op jit(solution)/shard_map/all_to_all | solution.py:325
  518.7 5.3 convolution_convert_fusion.3
  526.1 27.3 %gain_sum.1 = f32[40,128]{1,0:T(8,128)} custom-call(f32[40,128]{1,0:T(8,128)} %bitcast.200), custom_call_target="tpu_custom_call" | custom-call | tf_op jit(solution)/shard_map/gain_sum/pallas_call | solution.py:301
  554.6 5.7 all-to-all-start.6
  568.4 5.8 all-to-all-done.6
  575.0 21.0 %collective-permute-done.1 = f32[108,1152]{1,0:T(8,128)} collective-permute-done((f32[108,1152]{1,0:T(8,128)}, f32[108,1152]{1,0:T(8,128)}, u32[]{:S(2)}, u32[]{:S(2)}) %collective-permute-start.1) | collective-permute-done | bytes 497696 | tf_op jit(solution)/shard_map/ppermute | solution.py:486
  (252 shorter events, 92.4 us)
Async XLA Ops:
  2.9 174.5 %collective-permute-start = (bf16[54,1152]{1,0:T(8,128)(2,1)}, bf16[54,1152]{1,0:T(8,128)(2,1)}, u32[]{:S(2)}, u32[]{:S(2)}) collective-permute-start(bf16[54,1152]{1,0:T(8,128)(2,1)} %constant_dynamic-slice_fusion), channel_id=1, source_target_pairs={{0,0},{1,16},{2,32},{3,48},{4,64},{5,80},{6,96},{7,112},{8,1},{9,1... | collective-permute-start | bytes 373256 | tf_op jit(solution)/shard_map/ppermute | solution.py:414
  6.1 12.7 %copy-start.58 = (s32[1,2,64]{2,1,0:T(2,128)S(1)}, s32[1,2,64]{2,1,0:T(2,128)}, u32[]{:S(2)}) copy-start(s32[1,2,64]{2,1,0:T(2,128)} %param.15) | copy-start | bytes 1540
  6.1 12.8 %copy-start.9 = (bf16[1,2,64,1152]{3,2,1,0:T(8,128)(2,1)S(1)}, bf16[1,2,64,1152]{3,2,1,0:T(8,128)(2,1)}, u32[]{:S(2)}) copy-start(bf16[1,2,64,1152]{3,2,1,0:T(8,128)(2,1)} %param.14) | copy-start | bytes 884740
  9.2 114.0 %all-to-all-start = ((bf16[8,144,432]{2,1,0:T(8,128)(2,1)}), bf16[8,144,432]{2,1,0:T(8,128)(2,1)}, u32[]{:S(2)}, u32[]{:S(2)}) async-start(bf16[8,144,432]{2,1,0:T(8,128)(2,1)} %broadcast_in_dim.27), calls=%async_computation | async-start | bytes 2359296 | tf_op jit(solution)/shard_map/all_to_all | solution.py:325
  18.8 44.9 %copy-start.59 = (f32[128]{0:T(128)}, f32[128]{0:T(128)S(1)}, u32[]{:S(2)}) copy-start(f32[128]{0:T(128)S(1)} %multiply_power_fusion) | copy-start | bytes 1540
  18.9 40.9 %copy-start.36 = (f32[1152]{0:T(1024)S(1)}, f32[1152]{0:T(1024)}, u32[]{:S(2)}) copy-start(f32[1152]{0:T(1024)} %param.20) | copy-start | bytes 13828
  62.7 29.0 %copy-start.6 = (f32[128,1536]{1,0:T(8,128)}, f32[128,1536]{1,0:T(8,128)S(1)}, u32[]{:S(2)}) copy-start(f32[128,1536]{1,0:T(8,128)S(1)} %fusion.76) | copy-start | bytes 2359300
  62.9 27.9 %copy-start.4 = (f32[128,1024]{1,0:T(8,128)}, f32[128,1024]{1,0:T(8,128)S(1)}, u32[]{:S(2)}) copy-start(f32[128,1024]{1,0:T(8,128)S(1)} %slice.109) | copy-start | bytes 1572868
  62.9 25.7 %copy-start.61 = (f32[128]{0:T(128)}, f32[128]{0:T(128)S(1)}, u32[]{:S(2)}) copy-start(f32[128]{0:T(128)S(1)} %convert_element_type.131) | copy-start | bytes 1540
  62.9 25.7 %copy-start.53 = (f32[128]{0:T(128)}, f32[128]{0:T(128)S(1)}, u32[]{:S(2)}) copy-start(f32[128]{0:T(128)S(1)} %add_rsqrt_fusion.5) | copy-start | bytes 1540
  64.0 26.9 %copy-start.20 = (f32[128,128]{1,0:T(8,128)}, f32[128,128]{1,0:T(8,128)S(1)}, u32[]{:S(2)}) copy-start(f32[128,128]{1,0:T(8,128)S(1)} %get-tuple-element.50) | copy-start | bytes 196612
  64.0 26.9 %copy-start.22 = (f32[128,128]{1,0:T(8,128)}, f32[128,128]{1,0:T(8,128)S(1)}, u32[]{:S(2)}) copy-start(f32[128,128]{1,0:T(8,128)S(1)} %get-tuple-element.51) | copy-start | bytes 196612
  125.3 52.1 %all-to-all-start.1 = ((bf16[8,144,432]{2,1,0:T(8,128)(2,1)}), bf16[8,144,432]{2,1,0:T(8,128)(2,1)}, u32[]{:S(2)}, u32[]{:S(2)}) async-start(bf16[8,144,432]{2,1,0:T(8,128)(2,1)} %broadcast_in_dim.28), calls=%async_computation.1 | async-start | bytes 2359296 | tf_op jit(solution)/shard_map/all_to_all | solution.py:325
  179.3 22.9 %all-to-all-start.2 = ((bf16[8,54,1152]{2,1,0:T(8,128)(2,1)}), bf16[8,54,1152]{2,1,0:T(8,128)(2,1)}, u32[]{:S(2)}, u32[]{:S(2)}) async-start(bf16[8,54,1152]{2,1,0:T(8,128)(2,1)} %broadcast_in_dim.29), calls=%async_computation.2 | async-start | bytes 2064384 | tf_op jit(solution)/shard_map/all_to_all | solution.py:325
  300.1 19.3 %slice-start = ((s8[4718592]{0:T(1024)(128)(4,1)}), s8[524288]{0:T(1024)(128)(4,1)S(1)}, s32[]{:S(2)}) async-start(s8[4718592]{0:T(1024)(128)(4,1)} %bitcast.172), calls=%async_computation.7 | async-start | bytes 1048576
  389.5 23.2 %copy-start.60 = (f32[128]{0:T(128)S(1)}, f32[128]{0:T(128)}, u32[]{:S(2)}) copy-start(f32[128]{0:T(128)} %copy-done.59) | copy-start | bytes 1540
  389.5 23.2 %copy-start.62 = (f32[128]{0:T(128)S(1)}, f32[128]{0:T(128)}, u32[]{:S(2)}) copy-start(f32[128]{0:T(128)} %copy-done.61) | copy-start | bytes 1540
  389.5 24.4 %copy-start.14 = (bf16[16,8,4,256]{3,1,2,0:T(8,128)(2,1)S(1)}, bf16[16,8,4,256]{3,1,2,0:T(8,128)(2,1)}, u32[]{:S(2)}) copy-start(bf16[16,8,4,256]{3,1,2,0:T(8,128)(2,1)} %copy-done.13) | copy-start | bytes 786436
  421.0 35.1 %copy-start.45 = (f32[1,2,4,128]{3,1,2,0:T(2,128)S(1)}, f32[1,2,4,128]{3,1,2,0:T(2,128)}, u32[]{:S(2)}) copy-start(f32[1,2,4,128]{3,1,2,0:T(2,128)} %copy.117) | copy-start | bytes 12292
  421.9 36.0 %copy-start.3 = (bf16[8,2,72,1536]{3,2,1,0:T(8,128)(2,1)S(1)}, bf16[8,2,72,1536]{3,2,1,0:T(8,128)(2,1)}, u32[]{:S(2)}) copy-start(bf16[8,2,72,1536]{3,2,1,0:T(8,128)(2,1)} %weight_gather.2) | copy-start | bytes 10616836
  448.6 49.0 %all-to-all-start.4 = ((bf16[8,8,1152]{2,1,0:T(8,128)(2,1)}), bf16[8,8,1152]{2,1,0:T(8,128)(2,1)}, u32[]{:S(2)}, u32[]{:S(2)}) async-start(bf16[8,8,1152]{2,1,0:T(8,128)(2,1)} %convert_bitcast_fusion), calls=%async_computation.4 | async-start | bytes 294912 | tf_op jit(solution)/shard_map/all_to_all | solution.py:325
  464.1 40.7 %copy-start.19 = (bf16[432,1152]{1,0:T(8,128)(2,1)S(1)}, bf16[432,1152]{1,0:T(8,128)(2,1)}, u32[]{:S(2)}) copy-start(bf16[432,1152]{1,0:T(8,128)(2,1)} %convolution_convert_fusion.5) | copy-start | bytes 2985988
  497.6 14.2 %all-to-all-start.3 = ((bf16[8,12,1152]{2,1,0:T(8,128)(2,1)}), bf16[8,12,1152]{2,1,0:T(8,128)(2,1)S(1)}, u32[]{:S(2)}, u32[]{:S(2)}) async-start(bf16[8,12,1152]{2,1,0:T(8,128)(2,1)} %reshape.380), calls=%async_computation.3 | async-start | bytes 589824 | tf_op jit(solution)/shard_map/all_to_all | solution.py:325
  511.8 42.8 %all-to-all-start.5 = ((bf16[8,108,1152]{2,1,0:T(8,128)(2,1)}), bf16[8,108,1152]{2,1,0:T(8,128)(2,1)}, u32[]{:S(2)}, u32[]{:S(2)}) async-start(bf16[8,108,1152]{2,1,0:T(8,128)(2,1)} %convert_element_type.158), calls=%async_computation.5 | async-start | bytes 4128768 | tf_op jit(solution)/shard_map/all_to_all | solution.py:325
  524.1 29.4 %copy-start.64 = (f32[128]{0:T(128)S(1)}, f32[128]{0:T(128)}, u32[]{:S(2)}) copy-start(f32[128]{0:T(128)} %get-tuple-element.21) | copy-start | bytes 1540
  524.1 29.4 %copy-start.8 = (f32[128,1152]{1,0:T(8,128)S(1)}, f32[128,1152]{1,0:T(8,128)}, u32[]{:S(2)}) copy-start(f32[128,1152]{1,0:T(8,128)} %copy-done.7) | copy-start | bytes 1769476
  524.1 29.4 %copy-start.12 = (bf16[1,2,64,1152]{3,2,1,0:T(8,128)(2,1)S(1)}, bf16[1,2,64,1152]{3,2,1,0:T(8,128)(2,1)}, u32[]{:S(2)}) copy-start(bf16[1,2,64,1152]{3,2,1,0:T(8,128)(2,1)} %param.14) | copy-start | bytes 884740
  524.1 29.4 %copy-start.24 = (f32[128,1152]{1,0:T(8,128)S(1)}, f32[128,1152]{1,0:T(8,128)}, u32[]{:S(2)}) copy-start(f32[128,1152]{1,0:T(8,128)} %get-tuple-element.62) | copy-start | bytes 1769476
  524.1 29.4 %copy-start.63 = (f32[128]{0:T(128)S(1)}, f32[128]{0:T(128)}, u32[]{:S(2)}) copy-start(f32[128]{0:T(128)} %rsqrt.58) | copy-start | bytes 1540
  554.6 19.6 %all-to-all-start.6 = ((bf16[8,54,1152]{2,1,0:T(8,128)(2,1)}), bf16[8,54,1152]{2,1,0:T(8,128)(2,1)S(1)}, u32[]{:S(2)}, u32[]{:S(2)}) async-start(bf16[8,54,1152]{2,1,0:T(8,128)(2,1)} %reshape.383), calls=%async_computation.6 | async-start | bytes 2064384 | tf_op jit(solution)/shard_map/all_to_all | solution.py:325
  560.3 37.6 %copy-start.1 = (bf16[864,1152]{1,0:T(8,128)(2,1)S(1)}, bf16[864,1152]{1,0:T(8,128)(2,1)}, u32[]{:S(2)}) copy-start(bf16[864,1152]{1,0:T(8,128)(2,1)} %param.19) | copy-start | bytes 5971972
  563.6 32.4 %collective-permute-start.1 = (f32[108,1152]{1,0:T(8,128)}, f32[108,1152]{1,0:T(8,128)}, u32[]{:S(2)}, u32[]{:S(2)}) collective-permute-start(f32[108,1152]{1,0:T(8,128)} %convert_reduce_fusion), channel_id=1, source_target_pairs={{0,0},{1,1},{2,2},{3,3},{4,64},{5,65},{6,66},{7,67},{8,4},{9,5},{1... | collective-permute-start | bytes 1493000 | tf_op jit(solution)/shard_map/ppermute | solution.py:486
  (45 other events, 137.2 us)

commit v3 on v1

--- a/solution.py
+++ b/solution.py
@@ -1,7 +1,13 @@
+import functools
+
 import jax
 import jax.numpy as jnp
 from jax import lax
+from jax.experimental import pallas as pl
+from jax.experimental.pallas import tpu as pltpu
 from jax.sharding import PartitionSpec as P
+
+MESH = pl.DeviceIdType.MESH
 
 D = 1152
 FF = 6912
@@ -83,8 +89,390 @@
     return jnp.dot(left_rows, pieces, preferred_element_type=jnp.float32)
 
 
-def ctx_gather(rows):
-    return lax.all_gather(rows, "ctx", axis=0, tiled=True)
+def meet(axis_peers):
+    barrier = pltpu.get_barrier_semaphore()
+    for peer in axis_peers:
+        pl.semaphore_signal(barrier, inc=1, device_id=peer, device_id_type=MESH)
+    pl.semaphore_wait(barrier, len(axis_peers))
+
+
+def remote(source, target, send_sem, recv_sem, peer):
+    return pltpu.make_async_remote_copy(
+        src_ref=source,
+        dst_ref=target,
+        send_sem=send_sem,
+        recv_sem=recv_sem,
+        device_id=peer,
+        device_id_type=MESH,
+    )
+
+
+LABELS = ("me", "up", "down", "far", "cross", "xup", "xdown", "xfar")
+
+
+def ctx_place():
+    me = lax.axis_index("ctx")
+    core = lax.rem(me, 2)
+    ring = lax.rem(me // 2, 4)
+    pair = me // 8
+    sibling = {"ctx": me + 1 - 2 * core}
+    rings = {"me": ring, "up": lax.rem(ring + 1, 4), "down": lax.rem(ring + 3, 4)}
+    rings["far"] = lax.rem(ring + 2, 4)
+    slots = {}
+    for name, where in rings.items():
+        slots[name] = pair * 8 + where * 2
+        slots["cross" if name == "me" else "x" + name] = (1 - pair) * 8 + where * 2
+    peers = {name: {"ctx": slots[name] + core} for name in ("up", "down", "cross")}
+    return core, sibling, slots, peers
+
+
+def fsdp_place():
+    ctx = lax.axis_index("ctx")
+    me = lax.axis_index("fsdp")
+    core = lax.rem(ctx, 2)
+    ring = me // 2
+    pair = lax.rem(me, 2)
+    sibling = {"ctx": ctx + 1 - 2 * core}
+    rings = {"me": ring, "up": lax.rem(ring + 1, 4), "down": lax.rem(ring + 3, 4)}
+    rings["far"] = lax.rem(ring + 2, 4)
+    slots = {}
+    for name, where in rings.items():
+        slots[name] = where * 2 + pair
+        slots["cross" if name == "me" else "x" + name] = where * 2 + 1 - pair
+    peers = {name: {"fsdp": slots[name]} for name in ("up", "down")}
+    peers["cross"] = {"ctx": lax.rem(ctx + 8, 16), "fsdp": slots["cross"]}
+    return core, sibling, slots, peers
+
+
+class Gather:
+    def __init__(self, kind, x_ref, o_ref, sems):
+        self.kind, self.o_ref = kind, o_ref
+        self.core, self.sibling, self.slots, self.peers = (
+            ctx_place() if kind == "ctx" else fsdp_place()
+        )
+        self.send, self.recv, self.pass_send, self.pass_recv, self.own_sem = sems
+        self.x_ref = x_ref
+        self.own = x_ref if kind == "ctx" else x_ref.at[self.core]
+        rows = self.own.shape[0]
+        first = (rows // 2 + 7) // 8 * 8
+        self.halves = (pl.ds(0, first), pl.ds(first, rows - first))
+        self.waits = []
+        self.arrivals = {}
+
+    def block(self, name, part=None):
+        if self.kind == "ctx":
+            index = (self.slots[name] + self.core,)
+        else:
+            index = (self.slots[name], self.core)
+        return self.o_ref.at[index if part is None else index + (part,)]
+
+    def forward(self, index, source, target, arrival, peer):
+        copy = remote(source, target, self.send.at[index], self.recv.at[arrival], self.peers[peer])
+        copy.start()
+        self.waits.append(copy)
+        return copy
+
+    def arrived(self, arrival, name, part=None):
+        block = self.block(name, part)
+        remote(block, block, self.send.at[0], self.recv.at[arrival], self.peers["up"]).wait_recv()
+
+    def hand_over(self, index, name, source=None):
+        block = self.block(name)
+        copy = remote(
+            block if source is None else source,
+            block,
+            self.pass_send.at[index],
+            self.pass_recv.at[index],
+            self.sibling,
+        )
+        copy.start()
+        self.arrivals[index] = copy
+
+    def stage(self, number):
+        if number == 0:
+            if self.kind == "ctx":
+                here = self.block("me")
+            else:
+                here = self.o_ref.at[self.slots["me"]]
+            self.local = pltpu.make_async_copy(self.x_ref, here, self.own_sem)
+            self.local.start()
+            self.forward(0, self.own, self.block("me"), 1, "up")
+            self.forward(1, self.own, self.block("me"), 0, "down")
+            self.forward(2, self.own, self.block("me"), 2, "cross")
+            if self.kind == "ctx":
+                self.hand_over(0, "me", self.own)
+        elif number == 1:
+            self.arrived(1, "down")
+            part = self.block("down", self.halves[0])
+            self.forward(3, part, part, 3, "up")
+            self.hand_over(1, "down")
+            self.arrived(0, "up")
+            part = self.block("up", self.halves[1])
+            self.forward(4, part, part, 4, "down")
+            self.hand_over(2, "up")
+        elif number == 2:
+            self.arrived(2, "cross")
+            block = self.block("cross")
+            self.forward(5, block, block, 5, "up")
+            self.forward(6, block, block, 6, "down")
+            self.hand_over(3, "cross")
+        elif number == 3:
+            self.arrived(3, "far", self.halves[0])
+            self.arrived(4, "far", self.halves[1])
+            block = self.block("far")
+            self.forward(7, block, block, 7, "cross")
+            self.hand_over(4, "far")
+        elif number == 4:
+            self.arrived(5, "xdown")
+            self.hand_over(5, "xdown")
+            self.arrived(6, "xup")
+            self.hand_over(6, "xup")
+        elif number == 5:
+            self.arrived(7, "xfar")
+            self.hand_over(7, "xfar")
+        else:
+            self.local.wait()
+            for copy in self.waits:
+                copy.wait_send()
+            for copy in self.arrivals.values():
+                copy.wait()
+
+
+def gather_body(kinds, *refs):
+    count = len(kinds)
+    inputs, outputs, sems = refs[:count], refs[count : 2 * count], refs[2 * count :]
+    jobs = [
+        Gather(kind, inputs[i], outputs[i], sems[5 * i : 5 * i + 5])
+        for i, kind in enumerate(kinds)
+    ]
+    greeted = [jobs[0].sibling]
+    for i, job in enumerate(jobs):
+        if job.kind not in kinds[:i]:
+            greeted += [job.peers[name] for name in ("up", "down", "cross")]
+    meet(greeted)
+    for number in range(7):
+        for job in jobs:
+            job.stage(number)
+
+
+def gather(kinds, arrays, collective_id):
+    shaped, shapes = [], []
+    for kind, array in zip(kinds, arrays):
+        rows, width = array.shape
+        if kind == "ctx":
+            shaped.append(array)
+            shapes.append((lax.axis_size("ctx"), rows, width))
+        else:
+            shaped.append(array.reshape(2, rows // 2, width))
+            shapes.append((lax.axis_size("fsdp"), 2, rows // 2, width))
+    gathered = pl.pallas_call(
+        functools.partial(gather_body, kinds),
+        out_shape=[jax.ShapeDtypeStruct(shape, jnp.bfloat16) for shape in shapes],
+        in_specs=[pl.BlockSpec(memory_space=pltpu.VMEM)] * len(kinds),
+        out_specs=[pl.BlockSpec(memory_space=pl.ANY)] * len(kinds),
+        scratch_shapes=([pltpu.SemaphoreType.DMA((8,))] * 4 + [pltpu.SemaphoreType.DMA])
+        * len(kinds),
+        compiler_params=pltpu.CompilerParams(collective_id=collective_id, has_side_effects=True),
+        name="gather_" + "_".join(kinds),
+    )(*shaped)
+    return [array.reshape(-1, array.shape[-1]) for array in gathered]
+
+
+def scatter_body(
+    rows, p_ref, o_ref, near, sums, held, near_send, near_recv, send, recv
+):
+    core, sibling, slots, peers = ctx_place()
+    meet([sibling] + [peers[name] for name in ("up", "down", "cross")])
+    count = p_ref.shape[1]
+    half = count // 2
+    halves = (pl.ds(0, half), pl.ds(half, half))
+    order = ("xfar", "xup", "xdown", "up", "down", "far", "cross", "me")
+    number = {name: i for i, name in enumerate(LABELS)}
+    first = {}
+    for name in order:
+        i = number[name]
+        first[name] = remote(
+            p_ref.at[slots[name] + 1 - core],
+            near.at[i],
+            near_send.at[i],
+            near_recv.at[i],
+            sibling,
+        )
+        first[name].start()
+
+    def add_up(name, target, start, stop, extras=()):
+        i = number[name]
+
+        @pl.loop(start // rows, stop // rows)
+        def _(step):
+            part = pl.ds(pl.multiple_of(step * rows, rows), rows)
+            total = p_ref[slots[name] + core, part, :].astype(jnp.float32)
+            total = total + near[i, part, :].astype(jnp.float32)
+            for extra in extras:
+                total = total + held[extra, part, :].astype(jnp.float32)
+            if target is None:
+                sums[i, part, :] = total.astype(jnp.bfloat16)
+            else:
+                target[part, :] = total
+
+    started = []
+
+    def push(index, name, slot, arrival, peer, part=None):
+        i = number[name]
+        source = sums.at[i] if part is None else sums.at[i, part]
+        target = held.at[slot] if part is None else held.at[slot, part]
+        copy = remote(source, target, send.at[index], recv.at[arrival], peers[peer])
+        copy.start()
+        started.append(copy)
+
+    def arrived(arrival, slot, part=None):
+        block = held.at[slot] if part is None else held.at[slot, part]
+        remote(block, block, send.at[0], recv.at[arrival], peers["up"]).wait_recv()
+
+    first["xfar"].wait_recv()
+    add_up("xfar", None, 0, count)
+    first["xup"].wait_recv()
+    add_up("xup", None, 0, count)
+    push(0, "xfar", 0, 0, "cross")
+    first["xdown"].wait_recv()
+    add_up("xdown", None, 0, count)
+    push(1, "xup", 2, 2, "up")
+    first["up"].wait_recv()
+    add_up("up", None, half, count)
+    push(2, "xdown", 1, 1, "down")
+    first["down"].wait_recv()
+    add_up("down", None, 0, half)
+    push(3, "up", 5, 5, "up", halves[1])
+    first["far"].wait_recv()
+    push(4, "down", 4, 4, "down", halves[0])
+    arrived(0, 0)
+    add_up("far", None, 0, half, (0,))
+    add_up("far", None, half, count, (0,))
+    push(5, "far", 3, 3, "up", halves[0])
+    push(6, "far", 3, 8, "down", halves[1])
+    first["cross"].wait_recv()
+    arrived(1, 1)
+    arrived(2, 2)
+    add_up("cross", None, 0, count, (1, 2))
+    arrived(3, 3, halves[0])
+    add_up("up", None, 0, half, (3,))
+    push(7, "cross", 6, 6, "cross")
+    arrived(8, 3, halves[1])
+    add_up("down", None, half, count, (3,))
+    push(8, "up", 5, 7, "up", halves[0])
+    first["me"].wait_recv()
+    push(9, "down", 4, 9, "down", halves[1])
+    arrived(6, 6)
+    arrived(5, 5, halves[1])
+    arrived(4, 4, halves[0])
+    arrived(7, 5, halves[0])
+    arrived(9, 4, halves[1])
+    add_up("me", o_ref, 0, count, (4, 5, 6))
+    for name in order:
+        first[name].wait_send()
+    for copy in started:
+        copy.wait_send()
+
+
+def ctx_scatter(partial, collective_id):
+    members = lax.axis_size("ctx")
+    width = partial.shape[-1]
+    blocks = partial.astype(jnp.bfloat16).reshape(members, -1, width)
+    count = blocks.shape[1]
+
+    def buffer(number):
+        return pltpu.VMEM((number, count, width), jnp.bfloat16)
+
+    return pl.pallas_call(
+        functools.partial(scatter_body, 16),
+        out_shape=jax.ShapeDtypeStruct((count, width), jnp.float32),
+        in_specs=[pl.BlockSpec(memory_space=pltpu.VMEM)],
+        out_specs=pl.BlockSpec(memory_space=pltpu.VMEM),
+        scratch_shapes=[buffer(8), buffer(8), buffer(7)]
+        + [pltpu.SemaphoreType.DMA((8,))] * 2
+        + [pltpu.SemaphoreType.DMA((10,))] * 2,
+        compiler_params=pltpu.CompilerParams(collective_id=collective_id, has_side_effects=True),
+        name="ctx_scatter",
+    )(blocks)
+
+
+def final_body(
+    ctx_size, fsdp_size, x_ref, w_ref, o_ref, g_ref, held, subtotal, others, blocks, *sems
+):
+    send, recv, send2, recv2, send3, recv3 = sems
+    ctx = lax.axis_index("ctx")
+    fsdp = lax.axis_index("fsdp")
+    ctx_peers = [{"ctx": ctx ^ r} for r in range(1, ctx_size)]
+    fsdp_peers = [{"fsdp": fsdp ^ r} for r in range(1, fsdp_size)]
+    meet(ctx_peers + fsdp_peers)
+    held[ctx] = x_ref[...]
+    copies = []
+    for r in range(1, ctx_size):
+        copies.append(remote(x_ref, held.at[ctx], send.at[r], recv.at[r], ctx_peers[r - 1]))
+        copies[-1].start()
+    pieces = []
+    for r in range(1, fsdp_size):
+        pieces.append(
+            remote(w_ref.at[fsdp ^ r], blocks.at[r], send3.at[r], recv3.at[r], fsdp_peers[r - 1])
+        )
+        pieces[-1].start()
+    for copy in copies:
+        copy.wait()
+    total = held[0]
+    for i in range(1, ctx_size):
+        total = total + held[i]
+    subtotal[...] = total
+    others[fsdp] = total
+    copies = []
+    for r in range(1, fsdp_size):
+        copies.append(
+            remote(subtotal, others.at[fsdp], send2.at[r], recv2.at[r], fsdp_peers[r - 1])
+        )
+        copies[-1].start()
+    for copy in pieces:
+        copy.wait()
+    piece = w_ref[fsdp].astype(jnp.float32)
+    for r in range(1, fsdp_size):
+        piece = piece + blocks[r].astype(jnp.float32)
+    g_ref[...] = piece
+    for copy in copies:
+        copy.wait()
+    total = others[0]
+    for i in range(1, fsdp_size):
+        total = total + others[i]
+    o_ref[...] = total
+
+
+def final_sum(vector, weights, collective_id):
+    ctx_size = lax.axis_size("ctx")
+    fsdp_size = lax.axis_size("fsdp")
+    rows = vector.reshape(-1, 128)
+    gains, sums = pl.pallas_call(
+        functools.partial(final_body, ctx_size, fsdp_size),
+        out_shape=[
+            jax.ShapeDtypeStruct(rows.shape, jnp.float32),
+            jax.ShapeDtypeStruct(weights.shape[1:], jnp.float32),
+        ],
+        in_specs=[pl.BlockSpec(memory_space=pltpu.VMEM)] * 2,
+        out_specs=[pl.BlockSpec(memory_space=pltpu.VMEM)] * 2,
+        scratch_shapes=[
+            pltpu.VMEM((ctx_size,) + rows.shape, jnp.float32),
+            pltpu.VMEM(rows.shape, jnp.float32),
+            pltpu.VMEM((fsdp_size,) + rows.shape, jnp.float32),
+            pltpu.VMEM(weights.shape, jnp.bfloat16),
+        ]
+        + [pltpu.SemaphoreType.DMA((ctx_size,))] * 2
+        + [pltpu.SemaphoreType.DMA((fsdp_size,))] * 4,
+        compiler_params=pltpu.CompilerParams(collective_id=collective_id, has_side_effects=True),
+        name="final_sum",
+    )(rows, weights)
+    return gains.reshape(-1), sums
+
+
+def spread(shard, axis_name):
+    members = lax.axis_size(axis_name)
+    copies = jnp.broadcast_to(shard[None], (members,) + shard.shape)
+    return swap_blocks(copies, axis_name).reshape(members * shard.shape[0], shard.shape[1])
 
 
 def swap_blocks(blocks, axis_name):
@@ -175,20 +563,8 @@
     score_scale = HEAD_DIM ** (-0.5)
     part = FF // ctx_size
     piece = part // fsdp_size
-    qkv_rows = qkv_weight.shape[0] // ctx_size
-    out_rows = out_weight.shape[0] // ctx_size
-    qkv_full = lax.all_gather(
-        lax.dynamic_slice_in_dim(qkv_weight, ctx_index * qkv_rows, qkv_rows, 0),
-        ("fsdp", "ctx"),
-        axis=0,
-        tiled=True,
-    )
-    out_full = lax.all_gather(
-        lax.dynamic_slice_in_dim(out_weight, ctx_index * out_rows, out_rows, 0),
-        ("fsdp", "ctx"),
-        axis=0,
-        tiled=True,
-    )
+    padded = (part + 127) // 128 * 128
+    (qkv_full,) = gather(("fsdp",), (qkv_weight,), 1)
     down_piece = lax.ppermute(
         lax.dynamic_slice_in_dim(down_weight, ctx_index * piece, piece, 0),
         ("ctx", "fsdp"),
@@ -198,18 +574,17 @@
             for f in range(fsdp_size)
         ],
     )
-    down_part = lax.all_gather(down_piece, "fsdp", axis=0, tiled=True)
-    gate_part_w = lax.all_gather(
-        lax.dynamic_slice_in_dim(gate_up_weight, ctx_index * part, part, 1),
+    down_part = jnp.pad(spread(down_piece, "fsdp"), ((0, padded - part), (0, 0)))
+    widen = ((0, 0), (0, padded - part))
+    gate_up_w = spread(
+        jnp.concatenate(
+            [
+                jnp.pad(lax.dynamic_slice_in_dim(gate_up_weight, first, part, 1), widen)
+                for first in (ctx_index * part, FF + ctx_index * part)
+            ],
+            axis=1,
+        ),
         "fsdp",
-        axis=0,
-        tiled=True,
-    )
-    up_part_w = lax.all_gather(
-        lax.dynamic_slice_in_dim(gate_up_weight, FF + ctx_index * part, part, 1),
-        "fsdp",
-        axis=0,
-        tiled=True,
     )
     resid_in = block_input.reshape(row_count, D).astype(jnp.float32)
     scale_one = rms_scale(resid_in)
@@ -226,7 +601,9 @@
         query_raw * query_scale * scale_query, cosine[:, None, :], sine_part[:, None, :]
     ).astype(jnp.bfloat16)
     key_rows = rotate(key_raw * key_scale * scale_key, cosine, sine_part).astype(jnp.bfloat16)
-    key_value = ctx_gather(jnp.concatenate([key_rows, value_rows], axis=1))
+    key_value, out_full = gather(
+        ("ctx", "fsdp"), (jnp.concatenate([key_rows, value_rows], axis=1), out_weight), 2
+    )
     key_value = key_value.reshape(ctx_size, seq_count, seq_rows, 2 * HEAD_DIM)
     key_value = key_value.transpose(1, 0, 2, 3).reshape(seq_count, key_count, 2 * HEAD_DIM)
     key_all = key_value[:, :, :HEAD_DIM]
@@ -241,31 +618,40 @@
     middle = resid_in + projected * scale_two * scale_attn_out
     scale_three = rms_scale(middle)
     ff_input = (middle * scale_three * scale_ff_in).astype(jnp.bfloat16)
-    ff_all = ctx_gather(ff_input)
-    gate_part = add_product(ff_all, gate_part_w)
-    up_part = add_product(ff_all, up_part_w)
+    (ff_all,) = gather(("ctx",), (ff_input,), 3)
+    gate_up = add_product(ff_all, gate_up_w)
+    gate_part = gate_up[:, :padded]
+    up_part = gate_up[:, padded:]
     gelu_value, gelu_slope = gelu_parts(gate_part)
     activation = (gelu_value * up_part).astype(jnp.bfloat16)
-    down_out = scatter_sum(add_product(activation, down_part), "ctx")
+    down_out = ctx_scatter(add_product(activation, down_part), 6)
     scale_four = rms_scale(down_out)
     block_output = (middle + down_out * scale_four * scale_ff_out).astype(jnp.bfloat16)
     cotangent = grad_output.reshape(row_count, D).astype(jnp.float32)
     ff_out_grad = jnp.sum(cotangent * down_out * scale_four, axis=0)
     down_cot = norm_back(down_out, scale_four, scale_ff_out, cotangent).astype(jnp.bfloat16)
-    down_cot_all = ctx_gather(down_cot)
+    (down_cot_all,) = gather(("ctx",), (down_cot,), 4)
     act_cot = transposed_product(down_cot_all, down_part)
-    gate_cot = (act_cot * up_part * gelu_slope).astype(jnp.bfloat16)
-    up_cot = (act_cot * gelu_value).astype(jnp.bfloat16)
-    ff_input_cot = scatter_sum(
-        transposed_product(gate_cot, gate_part_w) + transposed_product(up_cot, up_part_w), "ctx"
-    )
-    gate_up_sum = scatter_sum(
+    gate_up_cot = jnp.concatenate(
+        [act_cot * up_part * gelu_slope, act_cot * gelu_value], axis=1
+    ).astype(jnp.bfloat16)
+    ff_input_cot = ctx_scatter(transposed_product(gate_up_cot, gate_up_w), 7)
+    wide_grad = transposed_left(gate_up_cot, ff_all).astype(jnp.bfloat16)
+    down_partial = transposed_left(activation, down_cot_all).astype(jnp.bfloat16)
+    ff_sums = scatter_sum(
         jnp.concatenate(
-            [transposed_left(gate_cot, ff_all), transposed_left(up_cot, ff_all)], axis=0
+            [
+                jnp.concatenate(
+                    [wide_grad[:part], wide_grad[padded : padded + part]], axis=0
+                ).reshape(fsdp_size, 2 * piece, D),
+                down_partial[:part].reshape(fsdp_size, piece, D),
+            ],
+            axis=1,
         ),
         "fsdp",
     )
-    down_grad = scatter_sum(transposed_left(activation, down_cot_all), "fsdp")
+    gate_up_sum = ff_sums[: 2 * piece]
+    down_grad = ff_sums[2 * piece :]
     half = fsdp_size // 2
     gate_up_grad = lax.ppermute(
         gate_up_sum,
@@ -297,7 +683,7 @@
     kv_partial = jnp.concatenate([key_cot, value_cot], axis=2).reshape(
         seq_count, ctx_size, seq_rows, 2 * HEAD_DIM
     )
-    kv_local = scatter_sum(kv_partial.transpose(1, 0, 2, 3), "ctx")
+    kv_local = ctx_scatter(kv_partial.transpose(1, 0, 2, 3), 8)
     key_cot_local = kv_local[:, :HEAD_DIM]
     value_cot_local = kv_local[:, HEAD_DIM:]
     query_back = rotate_back(
@@ -319,20 +705,32 @@
     attn_input_cot = transposed_product(qkv_cot, qkv_full)
     attn_in_grad = jnp.sum(attn_input_cot * resid_in * scale_one, axis=0)
     input_grad = middle_cot + norm_back(resid_in, scale_one, scale_attn_in, attn_input_cot)
-    qkv_sum = scatter_sum(scatter_sum(transposed_left(qkv_cot, attn_input), "ctx"), "fsdp")
-    out_grad = scatter_sum(
-        scatter_sum(transposed_left(attended_low, projected_cot), "ctx"), "fsdp"
+    qkv_partial = transposed_left(qkv_cot, attn_input).astype(jnp.bfloat16)
+    out_partial = transposed_left(attended_low, projected_cot).astype(jnp.bfloat16)
+    weight_sums = ctx_scatter(
+        jnp.concatenate(
+            [qkv_partial.reshape(ctx_size, -1, D), out_partial.reshape(ctx_size, -1, D)], axis=1
+        ),
+        9,
+    ).astype(jnp.bfloat16)
+    qkv_cut = qkv_partial.shape[0] // ctx_size
+    weight_blocks = jnp.concatenate(
+        [
+            weight_sums[:qkv_cut].reshape(fsdp_size, -1, D),
+            weight_sums[qkv_cut:].reshape(fsdp_size, -1, D),
+        ],
+        axis=1,
     )
     gains = jnp.concatenate(
         [attn_in_grad, attn_out_grad, ff_in_grad, ff_out_grad, query_gain_grad, key_gain_grad]
     )
-    gains = jnp.sum(lax.all_gather(gains, "ctx"), axis=0)
-    gains = jnp.sum(lax.all_gather(gains, "fsdp"), axis=0)
+    gains, weight_grads = final_sum(gains, weight_blocks, 11)
+    qkv_cut = qkv_cut // fsdp_size
     return (
         block_output.reshape(1, seq_count, seq_rows, D),
         input_grad.reshape(1, seq_count, seq_rows, D),
-        qkv_sum.T,
-        out_grad,
+        weight_grads[:qkv_cut].T,
+        weight_grads[qkv_cut:],
         gate_up_grad,
         down_grad,
         gains[:D],

time: 840 us -> 486 us (0.58)
  waiting for transfers between devices: 374 us -> 34.1 us
  Pallas kernels: 0 us -> 257 us
  blocking collectives: 236 us -> 0 us
  starting transfers between devices: 64.2 us -> 25.7 us
  between operations: 15.2 us -> 2.43 us
  other arithmetic: 31.6 us -> 43.1 us
  local copies, waits for them, and re-layouts: 36.1 us -> 46.5 us
    pallas_call x0 -> x9, Pallas kernels: none -> 257 us  [the longest x4 134 us: ctx_scatter(): pl.pallas_call(functools.partial(scatter_body, 16), out_shape=jax.ShapeDt...]
    all_gather x5 -> x0, waiting for transfers between devices: 196 us -> none  [the longest x1 68 us: on_device(): lax.all_gather(lax.dynamic_slice_in_dim(qkv_weight, ctx_index * qkv_rows,...]
    all_gather x5 -> x0, blocking collectives: 169 us -> none  [the longest x1 41.8 us: on_device(): lax.all_gather(lax.dynamic_slice_in_dim(gate_up_weight, ctx_index * part,...]
    all_to_all x8 -> x3, waiting for transfers between devices: 118 us -> 10.8 us  [swap_blocks(): lax.all_to_all(blocks, axis_name, split_axis=0, concat_axis=0, tiled=True)]
    all_to_all x1 -> x0, blocking collectives: 66.7 us -> none  [swap_blocks(): lax.all_to_all(blocks, axis_name, split_axis=0, concat_axis=0, tiled=True)]
    all_to_all x8 -> x3, starting transfers between devices: 57.7 us -> 20.3 us  [swap_blocks(): lax.all_to_all(blocks, axis_name, split_axis=0, concat_axis=0, tiled=True)]
    ppermute x1, waiting for transfers between devices: 59.7 us -> 23.4 us  [on_device(): lax.ppermute(gate_up_sum, ('ctx', 'fsdp'), [(c * fsdp_size + f, half * c...]
    reduce_sum x9 -> x1, other arithmetic: 16.4 us -> 2.4 us  [scatter_sum(): return jnp.sum(swap_blocks(blocks, axis_name).astype(jnp.float32), axis=0)]
  transfers between devices with their start and end apart: 15 -> 5, of which waited for: 12 -> 2; matrix products, arithmetic and copies ran while one was open for 10% -> 9% of each run, Pallas kernels for 0% -> 32%
where the time goes in v3:
time: 486 us; the launch traced here: 479 us
  Pallas kernels  257 us (53%)
  matrix products  70.2 us (14%)
  local copies, waits for them, and re-layouts  46.5 us (10%)
  other arithmetic  43.1 us (9%)
  waiting for transfers between devices  34.1 us (7%)
  starting transfers between devices  25.7 us (5%)
    pallas_call x4, Pallas kernels, ctx_scatter(): pl.pallas_call(functools.partial(scatter_body, 16), out_shape=jax.ShapeDt...  134 us
    pallas_call x4, Pallas kernels, gather(): pl.pallas_call(functools.partial(gather_body, kinds), out_shape=[jax.Shap...  106 us
    dot_general x4, matrix products, transposed_product(): lax.dot_general(right_rows, pieces, (((1,), (1,)), ((), ())), preferred_e...  24.1 us
    ppermute x1, waiting for transfers between devices, on_device(): lax.ppermute(gate_up_sum, ('ctx', 'fsdp'), [(c * fsdp_size + f, half * c...  23.4 us
    all_to_all x3, starting transfers between devices, swap_blocks(): lax.all_to_all(blocks, axis_name, split_axis=0, concat_axis=0, tiled=True)  20.3 us
    dot_general x4, matrix products, transposed_left(): lax.dot_general(left_rows, right_rows, (((0,), (0,)), ((), ())), preferre...  18.3 us
    pallas_call x1, Pallas kernels, final_sum(): pl.pallas_call(functools.partial(final_body, ctx_size, fsdp_size), out_sh...  17.4 us
    dot_general x2, matrix products, add_product(): return jnp.dot(left_rows, pieces, preferred_element_type=jnp.float32)  12.9 us
  transfers between devices with their start and end apart: 5, of which 2 were waited for; matrix products, arithmetic and copies ran while one was open for 9% of the time, Pallas kernels for 32%

profile of v3, /device:TPU:14, one launch (start us, length us, event | category | flops | bytes accessed | tf_op | source)
XLA Modules:
  0.0 479.3 jit_solution(16680037525270939100)
XLA Ops:
  2.2 3.2 collective-permute-start
  8.1 26.7 %gather_fsdp.1 = bf16[8,2,72,1536]{3,2,1,0:T(8,128)(2,1)} custom-call(bf16[2,72,1536]{2,1,0:T(8,128)(2,1)} %bitcast.185), custom_call_target="tpu_custom_call" | custom-call | tf_op jit(solution)/shard_map/gather_fsdp/pallas_call | solution.py:268
  34.9 2.7 fusion.87
  39.9 21.3 %gather_ctx_fsdp.1 = (bf16[16,128,512]{2,1,0:T(8,128)(2,1)}, bf16[8,2,64,1152]{3,2,1,0:T(8,128)(2,1)}) custom-call(bf16[128,512]{1,0:T(8,128)(2,1)} %pad_maximum_fusion.13.refs_0_, bf16[2,64,1152]{2,1,0:T(8,128)(2,1)} %bitcast.187), custom_call_target="tpu_custom_call" | custom-call | tf_op jit(solution)/shard_map/gather_ctx_fsdp/pallas_call | solution.py:268
  61.2 3.2 copy.95
  66.7 5.8 %all-to-all-start.1 = ((bf16[8,54,1152]{2,1,0:T(8,128)(2,1)}), bf16[8,54,1152]{2,1,0:T(8,128)(2,1)S(1)}, u32[]{:S(2)}, u32[]{:S(2)}) async-start(bf16[8,54,1152]{2,1,0:T(8,128)(2,1)} %broadcast_in_dim.30), calls=%async_computation.1 | async-start | bytes 2064384 | tf_op jit(solution)/shard_map/all_to_all | solution.py:479
  76.6 10.8 %all-to-all-done.1 = bf16[8,54,1152]{2,1,0:T(8,128)(2,1)S(1)} async-done(((bf16[8,54,1152]{2,1,0:T(8,128)(2,1)}), bf16[8,54,1152]{2,1,0:T(8,128)(2,1)S(1)}, u32[]{:S(2)}, u32[]{:S(2)}) %all-to-all-start.1) | async-done | bytes 995360 | tf_op jit(solution)/shard_map/all_to_all | solution.py:479
  89.1 7.2 %all-to-all-start = ((bf16[8,144,1024]{2,1,0:T(8,128)(2,1)}), bf16[8,144,1024]{2,1,0:T(8,128)(2,1)}, u32[]{:S(2)}, u32[]{:S(2)}) async-start(bf16[8,144,1024]{2,1,0:T(8,128)(2,1)} %broadcast_in_dim.25), calls=%async_computation | async-start | bytes 4718592 | tf_op jit(solution)/shard_map/all_to_all | solution.py:479
  96.4 4.3 fusion.86
  106.1 33.2 %gather_ctx.2 = bf16[16,128,1152]{2,1,0:T(8,128)(2,1)} custom-call(bf16[128,1152]{1,0:T(8,128)(2,1)} %multiply_convert_fusion.4.refs_0_), custom_call_target="tpu_custom_call" | custom-call | tf_op jit(solution)/shard_map/gather_ctx/pallas_call | solution.py:268
  146.3 8.4 %fusion.88 = f32[2048,1024]{0,1:T(8,128)S(1)} fusion(bf16[2048,1152]{1,0:T(8,128)(2,1)} %bitcast.156, bf16[1152,1024]{1,0:T(8,128)(2,1)} %bitcast.17), kind=kOutput, calls=%fused_computation.196 | convolution fusion | flops 4831838208 | bytes 15466496 | tf_op jit(solution)/shard_map/dot_general | solution.py:89
  156.7 4.5 convolution_convert_fusion.2
  161.2 31.1 %ctx_scatter.4 = f32[128,1152]{1,0:T(8,128)} custom-call(bf16[16,128,1152]{2,1,0:T(8,128)(2,1)} %bitcast.163), custom_call_target="tpu_custom_call" | custom-call | tf_op jit(solution)/shard_map/ctx_scatter/pallas_call | solution.py:386
  197.7 24.8 %gather_ctx.3 = bf16[16,128,1152]{2,1,0:T(8,128)(2,1)} custom-call(bf16[128,1152]{1,0:T(8,128)(2,1)} %get-tuple-element.45.refs_0_), custom_call_target="tpu_custom_call" | custom-call | tf_op jit(solution)/shard_map/gather_ctx/pallas_call | solution.py:268
  222.5 9.3 %fusion.6 = (bf16[2048,512]{0,1:T(8,128)(2,1)S(1)}, bf16[2048,512]{0,1:T(8,128)(2,1)S(1)}) fusion(f32[2048,1024]{0,1:T(8,128)} %copy-done.4, bf16[2048,1152]{1,0:T(8,128)(2,1)} %bitcast.160, bf16[432,1152]{1,0:T(8,128)(2,1)} %reshape.365), kind=kOutput, calls=%fused_computation.13 | convolution fusion | flops 2440036352 | bytes 18296832 | tf_op jit(solution)/shard_map/dot_general | solution.py:77
  231.8 10.5 %convolution_convert_fusion = bf16[2048,1152]{1,0:T(8,128)(2,1)} fusion(bf16[1152,1024]{1,0:T(8,128)(2,1)} %bitcast.17, bf16[2048,512]{0,1:T(8,128)(2,1)S(1)} %get-tuple-element.34, bf16[2048,512]{0,1:T(8,128)(2,1)S(1)} %get-tuple-element.33), kind=kOutput, calls=%fused_computation | convolution fusion | flops 4842586112 | bytes 11272192 | tf_op jit(solution)/shard_map/dot_general | solution.py:77
  242.4 32.2 %ctx_scatter.5 = f32[128,1152]{1,0:T(8,128)} custom-call(bf16[16,128,1152]{2,1,0:T(8,128)(2,1)} %bitcast.162), custom_call_target="tpu_custom_call" | custom-call | tf_op jit(solution)/shard_map/ctx_scatter/pallas_call | solution.py:386
  281.5 2.5 bitcast_convert_fusion
  287.8 2.7 copy.105
  290.5 3.3 copy.106
  293.7 17.6 %ctx_scatter.6 = f32[128,512]{1,0:T(8,128)} custom-call(bf16[16,128,512]{2,1,0:T(8,128)(2,1)} %bitcast.155), custom_call_target="tpu_custom_call" | custom-call | tf_op jit(solution)/shard_map/ctx_scatter/pallas_call | solution.py:386
  318.2 6.5 %fusion.89 = bf16[512,1152]{1,0:T(8,128)(2,1)} fusion(bf16[2048,512]{0,1:T(8,128)(2,1)S(1)} %copy-done.19, bf16[2048,1152]{1,0:T(8,128)(2,1)} %bitcast.161), kind=kOutput, calls=%fused_computation.197 | convolution fusion | flops 2415919104 | bytes 7995392 | tf_op jit(solution)/shard_map/dot_general | solution.py:83
  324.8 8.4 %convolution_convert_fusion.3 = bf16[1024,1152]{1,0:T(8,128)(2,1)} fusion(bf16[2048,1152]{1,0:T(8,128)(2,1)S(1)} %bitcast.159, bf16[2048,512]{0,1:T(8,128)(2,1)S(1)} %copy-done.74, bf16[2048,512]{0,1:T(8,128)(2,1)S(1)} %copy-done.72), kind=kOutput, calls=%fused_computation.18 | convolution fusion | flops 4841406464 | bytes 11272192 | tf_op jit(solution)/shard_map/dot_general | solution.py:83
  341.3 3.3 fusion.44
  346.9 2.5 reshape.380
  352.5 2.7 reshape.379
  355.3 4.0 pad_maximum_fusion.2
  359.2 7.3 %all-to-all-start.2 = ((bf16[8,162,1152]{2,1,0:T(8,128)(2,1)}), bf16[8,162,1152]{2,1,0:T(8,128)(2,1)}, u32[]{:S(2)}, u32[]{:S(2)}) async-start(bf16[8,162,1152]{2,1,0:T(8,128)(2,1)} %pad_maximum_fusion.2), calls=%async_computation.2 | async-start | bytes 6193152 | tf_op jit(solution)/shard_map/all_to_all | solution.py:479
  366.5 4.7 pad_maximum_fusion.p_ref
  371.2 53.0 %ctx_scatter.7 = f32[160,1152]{1,0:T(8,128)} custom-call(bf16[16,160,1152]{2,1,0:T(8,128)(2,1)} %pad_maximum_fusion.p_ref), custom_call_target="tpu_custom_call" | custom-call | tf_op jit(solution)/shard_map/ctx_scatter/pallas_call | solution.py:386
  426.7 17.4 %final_sum.1 = (f32[40,128]{1,0:T(8,128)}, f32[20,1152]{1,0:T(8,128)}) custom-call(f32[40,128]{1,0:T(8,128)} %bitcast.188, bf16[8,20,1152]{2,1,0:T(8,128)(2,1)} %pad_maximum_fusion.8.w_ref), custom_call_target="tpu_custom_call" | custom-call | tf_op jit(solution)/shard_map/final_sum/pallas_call | solution.py:450
  454.7 23.4 %collective-permute-done.1 = f32[108,1152]{1,0:T(8,128)S(1)} collective-permute-done((f32[108,1152]{1,0:T(8,128)S(1)}, f32[108,1152]{1,0:T(8,128)S(1)}, u32[]{:S(2)}, u32[]{:S(2)}) %collective-permute-start.1) | collective-permute-done | bytes 497696 | tf_op jit(solution)/shard_map/ppermute | solution.py:656
  (265 shorter events, 78.5 us)
Async XLA Ops:
  0.7 34.1 %copy-start.10 = (bf16[1,2,64,1152]{3,2,1,0:T(8,128)(2,1)S(1)}, bf16[1,2,64,1152]{3,2,1,0:T(8,128)(2,1)}, u32[]{:S(2)}) copy-start(bf16[1,2,64,1152]{3,2,1,0:T(8,128)(2,1)} %param.14) | copy-start | bytes 884740
  0.7 34.1 %copy-start.43 = (f32[1152]{0:T(1024)S(1)}, f32[1152]{0:T(1024)}, u32[]{:S(2)}) copy-start(f32[1152]{0:T(1024)} %param.20) | copy-start | bytes 13828
  2.2 63.4 %collective-permute-start = (bf16[54,1152]{1,0:T(8,128)(2,1)S(1)}, bf16[54,1152]{1,0:T(8,128)(2,1)S(1)}, u32[]{:S(2)}, u32[]{:S(2)}) collective-permute-start(bf16[54,1152]{1,0:T(8,128)(2,1)S(1)} %constant_dynamic-slice_fusion), channel_id=1, source_target_pairs={{0,0},{1,16},{2,32},{3,48},{4,64},{5,80},{6,96},{7,112},{8,1},{9,1... | collective-permute-start | bytes 373256 | tf_op jit(solution)/shard_map/ppermute | solution.py:568
  5.4 33.3 %copy-start.65 = (f32[128]{0:T(128)}, f32[128]{0:T(128)S(1)}, u32[]{:S(2)}) copy-start(f32[128]{0:T(128)S(1)} %multiply_power_fusion) | copy-start | bytes 1540
  37.6 26.8 %copy-start.7 = (f32[128,1536]{1,0:T(8,128)}, f32[128,1536]{1,0:T(8,128)S(1)}, u32[]{:S(2)}) copy-start(f32[128,1536]{1,0:T(8,128)S(1)} %fusion.87) | copy-start | bytes 2359300
  37.8 26.6 %copy-start.5 = (f32[128,1024]{1,0:T(8,128)}, f32[128,1024]{1,0:T(8,128)S(1)}, u32[]{:S(2)}) copy-start(f32[128,1024]{1,0:T(8,128)S(1)} %slice.153) | copy-start | bytes 1572868
  37.9 26.5 %copy-start.67 = (f32[128]{0:T(128)}, f32[128]{0:T(128)S(1)}, u32[]{:S(2)}) copy-start(f32[128]{0:T(128)S(1)} %convert_element_type.117) | copy-start | bytes 1540
  37.9 26.5 %copy-start.60 = (f32[128]{0:T(128)}, f32[128]{0:T(128)S(1)}, u32[]{:S(2)}) copy-start(f32[128]{0:T(128)S(1)} %add_rsqrt_fusion.5) | copy-start | bytes 1540
  38.6 57.7 %copy-start.36 = (pred[2,64,1024]{2,1,0:T(8,128)(4,1)}, pred[2,64,1024]{2,1,0:T(8,128)(4,1)S(1)}, u32[]{:S(2)}) copy-start(pred[2,64,1024]{2,1,0:T(8,128)(4,1)S(1)} %fusion.53) | copy-start | bytes 393220
  39.1 33.5 %copy-start.27 = (f32[128,128]{1,0:T(8,128)}, f32[128,128]{1,0:T(8,128)S(1)}, u32[]{:S(2)}) copy-start(f32[128,128]{1,0:T(8,128)S(1)} %get-tuple-element.60) | copy-start | bytes 196612
  39.1 33.5 %copy-start.29 = (f32[128,128]{1,0:T(8,128)}, f32[128,128]{1,0:T(8,128)S(1)}, u32[]{:S(2)}) copy-start(f32[128,128]{1,0:T(8,128)S(1)} %get-tuple-element.61) | copy-start | bytes 196612
  66.7 20.7 %all-to-all-start.1 = ((bf16[8,54,1152]{2,1,0:T(8,128)(2,1)}), bf16[8,54,1152]{2,1,0:T(8,128)(2,1)S(1)}, u32[]{:S(2)}, u32[]{:S(2)}) async-start(bf16[8,54,1152]{2,1,0:T(8,128)(2,1)} %broadcast_in_dim.30), calls=%async_computation.1 | async-start | bytes 2064384 | tf_op jit(solution)/shard_map/all_to_all | solution.py:479
  74.6 21.7 %copy-start.50 = (f32[2,64,4]{1,2,0:T(4,128)}, f32[2,64,4]{1,2,0:T(4,128)S(1)}, u32[]{:S(2)}) copy-start(f32[2,64,4]{1,2,0:T(4,128)S(1)} %get-tuple-element.64) | copy-start | bytes 6148
  89.1 57.2 %all-to-all-start = ((bf16[8,144,1024]{2,1,0:T(8,128)(2,1)}), bf16[8,144,1024]{2,1,0:T(8,128)(2,1)}, u32[]{:S(2)}, u32[]{:S(2)}) async-start(bf16[8,144,1024]{2,1,0:T(8,128)(2,1)} %broadcast_in_dim.25), calls=%async_computation | async-start | bytes 4718592 | tf_op jit(solution)/shard_map/all_to_all | solution.py:479
  290.5 22.6 %copy-start.66 = (f32[128]{0:T(128)S(1)}, f32[128]{0:T(128)}, u32[]{:S(2)}) copy-start(f32[128]{0:T(128)} %copy-done.65) | copy-start | bytes 1540
  290.5 22.6 %copy-start.68 = (f32[128]{0:T(128)S(1)}, f32[128]{0:T(128)}, u32[]{:S(2)}) copy-start(f32[128]{0:T(128)} %copy-done.67) | copy-start | bytes 1540
  290.5 23.8 %copy-start.21 = (bf16[2,16,64,512]{3,2,1,0:T(8,128)(2,1)S(1)}, bf16[2,16,64,512]{3,2,1,0:T(8,128)(2,1)}, u32[]{:S(2)}) copy-start(bf16[2,16,64,512]{3,2,1,0:T(8,128)(2,1)} %copy.95) | copy-start | bytes 6291460
  293.7 22.2 %copy-start.15 = (bf16[128,1152]{1,0:T(8,128)(2,1)S(1)}, bf16[128,1152]{1,0:T(8,128)(2,1)}, u32[]{:S(2)}) copy-start(bf16[128,1152]{1,0:T(8,128)(2,1)} %copy-done.14) | copy-start | bytes 884740
  293.7 22.2 %copy-start.17 = (bf16[16,8,4,256]{3,1,2,0:T(8,128)(2,1)S(1)}, bf16[16,8,4,256]{3,1,2,0:T(8,128)(2,1)}, u32[]{:S(2)}) copy-start(bf16[16,8,4,256]{3,1,2,0:T(8,128)(2,1)} %copy-done.16) | copy-start | bytes 786436
  359.2 87.5 %all-to-all-start.2 = ((bf16[8,162,1152]{2,1,0:T(8,128)(2,1)}), bf16[8,162,1152]{2,1,0:T(8,128)(2,1)}, u32[]{:S(2)}, u32[]{:S(2)}) async-start(bf16[8,162,1152]{2,1,0:T(8,128)(2,1)} %pad_maximum_fusion.2), calls=%async_computation.2 | async-start | bytes 6193152 | tf_op jit(solution)/shard_map/all_to_all | solution.py:479
  371.2 54.5 %copy-start.48 = (f32[5120]{0:T(1024)S(1)}, f32[5120]{0:T(1024)}, u32[]{:S(2)}) copy-start(f32[5120]{0:T(1024)} %custom-call) | copy-start | bytes 61444
  371.2 54.5 %copy-start.57 = (f32[1152]{0:T(1024)S(1)}, f32[1152]{0:T(1024)}, u32[]{:S(2)}) copy-start(f32[1152]{0:T(1024)} %get-tuple-element.28) | copy-start | bytes 13828
  371.2 54.6 %copy-start.47 = (f32[1152]{0:T(1024)S(1)}, f32[1152]{0:T(1024)}, u32[]{:S(2)}) copy-start(f32[1152]{0:T(1024)} %get-tuple-element.22) | copy-start | bytes 13828
  371.2 54.6 %copy-start.46 = (f32[1152]{0:T(1024)S(1)}, f32[1152]{0:T(1024)}, u32[]{:S(2)}) copy-start(f32[1152]{0:T(1024)} %get-tuple-element.20) | copy-start | bytes 13828
  371.2 54.6 %copy-start.45 = (f32[1152]{0:T(1024)S(1)}, f32[1152]{0:T(1024)}, u32[]{:S(2)}) copy-start(f32[1152]{0:T(1024)} %get-tuple-element.26) | copy-start | bytes 13828
  371.2 54.6 %copy-start.63 = (f32[256]{0:T(256)S(1)}, f32[256]{0:T(256)}, u32[]{:S(2)}) copy-start(f32[256]{0:T(256)} %get-tuple-element.24) | copy-start | bytes 3076
  424.3 21.3 %copy-start.9 = (f32[128,1152]{1,0:T(8,128)S(1)}, f32[128,1152]{1,0:T(8,128)}, u32[]{:S(2)}) copy-start(f32[128,1152]{1,0:T(8,128)} %copy-done.8) | copy-start | bytes 1769476
  424.3 21.3 %copy-start.12 = (bf16[1,2,64,1152]{3,2,1,0:T(8,128)(2,1)S(1)}, bf16[1,2,64,1152]{3,2,1,0:T(8,128)(2,1)}, u32[]{:S(2)}) copy-start(bf16[1,2,64,1152]{3,2,1,0:T(8,128)(2,1)} %param.14) | copy-start | bytes 884740
  424.3 21.3 %copy-start.31 = (f32[128,1152]{1,0:T(8,128)S(1)}, f32[128,1152]{1,0:T(8,128)}, u32[]{:S(2)}) copy-start(f32[128,1152]{1,0:T(8,128)} %get-tuple-element.70) | copy-start | bytes 1769476
  424.3 21.3 %copy-start.69 = (f32[128]{0:T(128)S(1)}, f32[128]{0:T(128)}, u32[]{:S(2)}) copy-start(f32[128]{0:T(128)} %rsqrt.58) | copy-start | bytes 1540
  445.7 33.2 %copy-start.1 = (bf16[864,1152]{1,0:T(8,128)(2,1)S(1)}, bf16[864,1152]{1,0:T(8,128)(2,1)}, u32[]{:S(2)}) copy-start(bf16[864,1152]{1,0:T(8,128)(2,1)} %param.19) | copy-start | bytes 5971972
  449.2 28.9 %collective-permute-start.1 = (f32[108,1152]{1,0:T(8,128)S(1)}, f32[108,1152]{1,0:T(8,128)S(1)}, u32[]{:S(2)}, u32[]{:S(2)}) collective-permute-start(f32[108,1152]{1,0:T(8,128)S(1)} %slice.172), channel_id=1, source_target_pairs={{0,0},{1,1},{2,2},{3,3},{4,64},{5,65},{6,66},{7,67},{8,4},{9,5},{1... | collective-permute-start | bytes 1493000 | tf_op jit(solution)/shard_map/ppermute | solution.py:656
  (50 other events, 254.9 us)
